TPU v7x, 128 devices: a whole 4x4x4 slice. The times are simulated.
128 devices in a mesh: lat: 8 (over y, core), lon: 16 (over z, x).
Axes of the slice: x: 4, y: 4, z: 4, core: 2. Of those that a mesh axis runs over, the one named last changes fastest.
Arguments:
- increment: float32 [2, 50, 128, 1024], P(None, None, 'lon', 'lat'), may hold values from -6 to 6
- residual: float32 [2, 50, 128, 1024], P(None, None, 'lon', 'lat'), may hold values from -21 to 21
- direction: float32 [2, 50, 128, 1024], P(None, None, 'lon', 'lat'), may hold values from -21 to 21
- diffusivity: float32 [2, 50, 128, 1024], P(None, None, 'lon', 'lat'), may hold values from 0.03 to 0.24
- deviation: float32 [2, 50, 128, 1024], P(None, None, 'lon', 'lat'), may hold values from 0.5 to 2
- stencil: int32 [16384, 128], P(('lat', 'lon')), may hold values from 0 to 51070, as said below
- bilinear: float32 [16384, 4, 128], P(('lat', 'lon')), may hold values from 0 to 1, as said below
- obs_weight: float32 [2, 16384, 128], P(None, ('lat', 'lon')), may hold values from 2 to 6
- block_owner: int32 [16384, 1], P(('lat', 'lon')), may hold values from 0 to 127; in each aligned block of 128 rows (0 to 127, 128 to 255, ...) at most 2 rows name the same one
- correlation: float32 [16384, 128], P(('lat', 'lon')), may hold values from -0.5 to 2, as said below
Outputs:
- next_increment: float32 [2, 50, 128, 1024], P(None, None, 'lon', 'lat')
- next_residual: float32 [2, 50, 128, 1024], P(None, None, 'lon', 'lat')
- next_direction: float32 [2, 50, 128, 1024], P(None, None, 'lon', 'lat')
Inputs may be any that keep to these rules, and one draw needn't show every extreme that they name: `stencil`: each entry is (l * 8 + i) * 128 + j for a level l, a longitude cell i < 7 and a latitude cell j < 127 of the block's tile, so that all four cells of the square lie in that tile. `bilinear`: the four weights of each observation are non-negative and sum to one. `block_owner`: among the 128 blocks of one tile no owner is named more than 2 times, and in every draw some tile names some owner exactly 2 times. `correlation`: each owner's 128 x 128 matrix is symmetric and positive definite.
All inputs are finite; a program needn't handle non-finite values.
Results may differ from a plain program's by a relative error of at most 0.0001.
Values sent between devices are 32-bit elements; how exact they have to be, the bound alone decides.
A program may use at most 64 MiB of HBM per device.

v0:
```python
import math

import jax
import jax.numpy as jnp
from jax import lax
from jax.sharding import PartitionSpec as P

STEPS = 4
CAP = 2


precise = lax.Precision.HIGHEST


def with_halo(value, sides, width, wrap):
    for axis, dim in sides:
        size, length = (lax.axis_size(axis), value.shape[dim])
        up = [(i, (i + 1) % size) for i in range(size if wrap else size - 1)]
        down = [(j, i) for i, j in up]
        last = lax.slice_in_dim(value, length - width, length, axis=dim)
        leading = lax.slice_in_dim(value, 0, width, axis=dim)
        before = lax.ppermute(last, axis, up)
        after = lax.ppermute(leading, axis, down)
        value = jnp.concatenate([before, value, after], axis=dim)
    return value


def rim_lat(field):
    return with_halo(field, (("lat", 3),), 1, False)


def rim_lon(field):
    return with_halo(field, (("lon", 2),), 1, True)


def face_coeffs(diffusivity):
    lat_wide = rim_lat(diffusivity)
    lon_wide = rim_lon(diffusivity)
    return (
        0.5 * (diffusivity + lat_wide[:, :, :, 2:]),
        0.5 * (diffusivity + lat_wide[:, :, :, :-2]),
        0.5 * (diffusivity + lon_wide[:, :, 2:, :]),
        0.5 * (diffusivity + lon_wide[:, :, :-2, :]),
    )


def diffuse(field, coeffs):
    north_face, south_face, east_face, west_face = coeffs
    for sweep in range(STEPS):
        lat_wide = rim_lat(field)
        lon_wide = rim_lon(field)
        field = (
            field
            + north_face * (lat_wide[:, :, :, 2:] - field)
            + south_face * (lat_wide[:, :, :, :-2] - field)
            + east_face * (lon_wide[:, :, 2:, :] - field)
            + west_face * (lon_wide[:, :, :-2, :] - field)
        )
    return field


def obs_groups(stencil, bilinear):
    block_count, obs_count = stencil.shape
    group = math.gcd(block_count, max(1, 1024 // obs_count))
    steps_count = block_count // group
    bases = stencil.reshape(steps_count, group * obs_count)
    corner_weights = jnp.transpose(bilinear.reshape(steps_count, group, 4, obs_count), (0, 2, 1, 3))
    return (bases, corner_weights.reshape(steps_count, 4, group * obs_count), steps_count)


def lat_weights(lat_base, first_weight, second_weight, lat_count):
    cells = jnp.arange(lat_count, dtype=jnp.int32)[:, None]
    return jnp.where(cells == lat_base[None, :], first_weight[None, :], 0.0) + jnp.where(
        cells == lat_base[None, :] + 1, second_weight[None, :], 0.0
    )


def block_maps(base, weights_four, row_count, lat_count):
    row_base = base // lat_count
    lat_base = base - row_base * lat_count
    rows = jnp.arange(row_count, dtype=jnp.int32)[:, None]
    near_rows = (rows == row_base[None, :]).astype(jnp.float32)
    far_rows = (rows == row_base[None, :] + 1).astype(jnp.float32)
    near_lat = lat_weights(lat_base, weights_four[0], weights_four[1], lat_count)
    far_lat = lat_weights(lat_base, weights_four[2], weights_four[3], lat_count)
    return (near_rows, far_rows, near_lat, far_lat)


def observe(field, stencil, bilinear, obs_weight):
    var_count, level_count, lon_count, lat_count = field.shape
    row_count = level_count * lon_count
    row_field = field.reshape(var_count, row_count, lat_count)
    bases, corner_weights, steps_count = obs_groups(stencil, bilinear)

    def one_group(pair):
        near_rows, far_rows, near_lat, far_lat = block_maps(pair[0], pair[1], row_count, lat_count)
        near_vals = jnp.einsum("vrj,jk->vrk", row_field, near_lat, precision=precise)
        far_vals = jnp.einsum("vrj,jk->vrk", row_field, far_lat, precision=precise)
        return jnp.sum(near_vals * near_rows[None] + far_vals * far_rows[None], axis=1)

    values = lax.map(one_group, (bases, corner_weights))
    values = jnp.transpose(values, (1, 0, 2)).reshape(obs_weight.shape)
    return obs_weight * values


def spread_back(weighted, stencil, bilinear, field_shape):
    var_count, level_count, lon_count, lat_count = field_shape
    row_count = level_count * lon_count
    bases, corner_weights, steps_count = obs_groups(stencil, bilinear)
    grouped = jnp.transpose(weighted.reshape(var_count, steps_count, -1), (1, 0, 2))

    def add_group(total, triple):
        base, weights_four, values = triple
        near_rows, far_rows, near_lat, far_lat = block_maps(
            base, weights_four, row_count, lat_count
        )
        near_part = jnp.einsum(
            "vrk,jk->vrj", near_rows[None] * values[:, None, :], near_lat, precision=precise
        )
        far_part = jnp.einsum(
            "vrk,jk->vrj", far_rows[None] * values[:, None, :], far_lat, precision=precise
        )
        return (total + near_part + far_part, None)

    start = jnp.zeros((var_count, row_count, lat_count), jnp.float32)
    total, unused = lax.scan(add_group, start, (bases, corner_weights, grouped))
    return total.reshape(field_shape)


def slots_of(block_owner, tile_count):
    targets = block_owner[:, 0]
    block_count = targets.shape[0]
    same_owner = (targets[:, None] == jnp.arange(tile_count, dtype=jnp.int32)[None, :]).astype(
        jnp.int32
    )
    order = jnp.arange(block_count, dtype=jnp.int32)
    lower = (order[:, None] > order[None, :]).astype(jnp.int32)
    earlier = jnp.dot(lower, same_owner)
    rank_within = jnp.sum(earlier * same_owner, axis=1)
    return targets * CAP + rank_within


def mix_blocks(values, correlation):
    return jnp.einsum("vsk,ik->vsi", values, correlation, precision=precise)


def shards(
    increment,
    residual,
    direction,
    diffusivity,
    deviation,
    stencil,
    bilinear,
    obs_weight,
    block_owner,
    correlation,
):
    lat_devices = lax.axis_size("lat")
    lon_devices = lax.axis_size("lon")
    tile_count = lat_devices * lon_devices
    coeffs = face_coeffs(diffusivity)

    def apply_diffusion(field):
        return diffuse(field, coeffs)

    slots = slots_of(block_owner, tile_count)
    slot_table = (slots[:, None] == jnp.arange(tile_count * CAP, dtype=jnp.int32)[None, :]).astype(
        jnp.float32
    )
    field_shape = direction.shape
    norm_now = lax.psum(jnp.sum(residual * residual), ("lat", "lon"))
    state_field = deviation * apply_diffusion(direction)
    observed = observe(state_field, stencil, bilinear, obs_weight)
    buffer = jnp.einsum("vbk,bs->vsk", observed, slot_table, precision=precise)
    returned = lax.all_to_all(
        mix_blocks(
            lax.all_to_all(buffer, ("lat", "lon"), split_axis=1, concat_axis=1, tiled=True),
            correlation,
        ),
        ("lat", "lon"),
        split_axis=1,
        concat_axis=1,
        tiled=True,
    )
    weighted = obs_weight * jnp.einsum("vsk,bs->vbk", returned, slot_table, precision=precise)
    spread_field = deviation * spread_back(weighted, stencil, bilinear, field_shape)
    image_field = direction + apply_diffusion(spread_field)
    curvature = lax.psum(jnp.sum(direction * image_field), ("lat", "lon"))
    step_size = norm_now / curvature
    increment = increment + step_size * direction
    residual = residual - step_size * image_field
    norm_next = lax.psum(jnp.sum(residual * residual), ("lat", "lon"))
    direction = residual + norm_next / norm_now * direction
    return (increment, residual, direction)


def solution(mesh):
    in_specs = (
        P(None, None, "lon", "lat"),
        P(None, None, "lon", "lat"),
        P(None, None, "lon", "lat"),
        P(None, None, "lon", "lat"),
        P(None, None, "lon", "lat"),
        P(("lat", "lon"), None),
        P(("lat", "lon"), None, None),
        P(None, ("lat", "lon"), None),
        P(("lat", "lon"), None),
        P(("lat", "lon"), None),
    )
    out_specs = (
        P(None, None, "lon", "lat"),
        P(None, None, "lon", "lat"),
        P(None, None, "lon", "lat"),
    )
    return jax.shard_map(shards, mesh=mesh, in_specs=in_specs, out_specs=out_specs, check_vma=False)
```

profile of v0, /device:TPU:1, one launch (start us, length us, event | category | flops | bytes accessed | tf_op | source)
XLA Modules:
  0.0 602.5 jit_solution(6678041378075305552)
XLA Ops:
  1.9 6.8 %collective-permute-start.4 = (f32[2,50,1,128]{3,2,1,0:T(1,128)S(1)}, f32[2,50,1,128]{3,2,1,0:T(1,128)S(1)}, u32[]{:S(2)}, u32[]{:S(2)}) collective-permute-start(f32[2,50,1,128]{3,2,1,0:T(1,128)S(1)} %get-tuple-element.235), channel_id=1, source_target_pairs={{1,0},{2,1},{3,2},{4,3},{5,4},{6,5},{7,6},{8,7},{9,8},{10,9},{11,1... | collective-permute-start | bytes 153608 | tf_op jit(solution)/shard_map/ppermute | solution.py:23
  13.1 5.1 collective-permute-start.5
  21.7 7.3 %collective-permute-done.1 = f32[2,50,8,1]{3,2,1,0:T(8,128)S(1)} collective-permute-done((f32[2,50,8,1]{3,2,1,0:T(8,128)S(1)}, f32[2,50,8,1]{3,2,1,0:T(8,128)S(1)}, u32[]{:S(2)}, u32[]{:S(2)}) %collective-permute-start.1) | collective-permute-done | bytes 3232 | tf_op jit(solution)/shard_map/ppermute | solution.py:23
  31.0 4.9 collective-permute-done.2
  35.8 4.4 collective-permute-start.3
  40.2 4.9 collective-permute-done.3
  46.0 5.2 collective-permute-start.10
  53.4 4.7 collective-permute-start.9
  58.0 3.7 collective-permute-done.8
  65.7 4.4 collective-permute-start.13
  70.1 5.1 collective-permute-start.14
  76.5 5.1 collective-permute-done.15
  84.4 4.3 collective-permute-start.17
  97.3 124.1 %while.25 = (s32[]{:T(128)}, f32[16,2,1024]{2,1,0:T(2,128)S(1)}, s32[16,1024]{1,0:T(8,128)S(1)}, f32[16,4,1024]{2,1,0:T(4,128)}, f32[2,400,128]{2,1,0:T(8,128)S(...) while((s32[]{:T(128)}, f32[16,2,1024]{2,1,0:T(2,128)S(1)}, s32[16,1024]{1,0:T(8,128)S(1)}, ...), condition=%wide.region_5.6_spmd, body=%wide.region_3.5_spmd.sunk | while | flops 2522825728 | bytes 14053541 | solution.py:101
  222.1 16.2 %all_to_all.10 = f32[2,256,128]{2,0,1:T(2,128)S(1)} all-to-all(f32[2,256,128]{2,0,1:T(2,128)S(1)} %copy.27), channel_id=1, replica_groups=mesh['lat'=8,'lon'=16] {'lat','lon'}, dimensions={1} | all-to-all | bytes 524288 | tf_op jit(solution)/shard_map/all_to_all | solution.py:178
  239.5 4.0 all-to-all-start.1
  243.6 11.5 %all-to-all-done.1 = f32[2,256,128]{2,0,1:T(2,128)S(1)} async-done(((f32[2,256,128]{2,0,1:T(2,128)}), f32[2,256,128]{2,0,1:T(2,128)S(1)}, u32[]{:S(2)}, u32[]{:S(2)}) %all-to-all-start.1) | async-done | bytes 262176 | tf_op jit(solution)/shard_map/all_to_all | solution.py:176
  256.1 148.6 %while.26 = (s32[]{:T(128)}, f32[2,400,128]{2,1,0:T(8,128)}, s32[16,1024]{1,0:T(8,128)S(1)}, f32[16,2,1024]{2,1,0:T(2,128)}, f32[16,4,1024]{2,1,0:T(4,128)}, /*index=5*/s32[]{:T(128)}, s32[]{:T(128)}, s32[]{}, s32[]{}, s32[]{}) while((s32[]{:T(128)}, f32[2,400,128]{2,1,0:T(8,128)}, s32[16,1024]{1,0:T(8,128)S(1)}, ...), condition=%wide.region_7.8_spmd.clone, body=%wide.region_6.7_spmd.clone.sunk | while | flops 2521496576 | bytes 8327343 | solution.py:126
  260.9 3.5 fusion.234
  266.3 3.8 fusion.232
  275.6 3.8 fusion.232
  285.0 3.8 fusion.232
  294.3 3.8 fusion.232
  303.7 3.8 fusion.232
  313.0 3.8 fusion.232
  322.4 3.8 fusion.232
  331.7 3.8 fusion.232
  335.7 3.5 fusion.234
  341.1 3.8 fusion.232
  350.4 3.8 fusion.232
  359.8 3.8 fusion.232
  369.1 3.8 fusion.232
  378.5 3.8 fusion.232
  387.8 3.8 fusion.232
  397.2 3.8 fusion.232
  401.1 3.5 fusion.234
  413.1 3.7 collective-permute-done.20
  418.7 4.2 collective-permute-start.26
  425.0 4.7 collective-permute-start.25
  429.7 3.7 collective-permute-done.24
  435.2 5.1 collective-permute-start.30
  442.5 4.7 collective-permute-start.29
  447.2 3.7 collective-permute-done.28
  455.1 4.4 collective-permute-start.33
  459.5 5.1 collective-permute-start.34
  465.8 5.1 collective-permute-done.35
  472.2 61.9 %all-reduce = (f32[]{:T(128)}, f32[]{:T(128)}) all-reduce(f32[]{:T(128)} %multiply_reduce_fusion.2, f32[]{:T(128)} %get-tuple-element.187), channel_id=1, replica_groups=mesh['lat'=8,'lon'=16] {'lat','lon'}, use_global_device_ids=true, to_apply=%region_1.0 | all-reduce | flops 2 | bytes 16 | tf_op jit(solution)/shard_map/psum | solution.py:172
  536.1 64.1 %psum.23 = f32[]{:T(128)} all-reduce(f32[]{:T(128)} %get-tuple-element.185), channel_id=1, replica_groups=mesh['lat'=8,'lon'=16] {'lat','lon'}, use_global_device_ids=true, to_apply=%region_11.12 | all-reduce | flops 1 | bytes 8 | tf_op jit(solution)/shard_map/psum | solution.py:193
  (341 shorter events, 262.5 us)
Async XLA Ops:
  0.6 237.6 %copy-start = (f32[128,128]{1,0:T(8,128)S(1)}, f32[128,128]{1,0:T(8,128)}, u32[]{:S(2)}) copy-start(f32[128,128]{1,0:T(8,128)} %param.23) | copy-start | bytes 196612
  0.6 12.3 %copy-start.2 = (f32[2,50,8,128]{3,2,1,0:T(8,128)S(1)}, f32[2,50,8,128]{3,2,1,0:T(8,128)}, u32[]{:S(2)}) copy-start(f32[2,50,8,128]{3,2,1,0:T(8,128)} %param.16) | copy-start | bytes 1228804
  1.9 43.2 %collective-permute-start.4 = (f32[2,50,1,128]{3,2,1,0:T(1,128)S(1)}, f32[2,50,1,128]{3,2,1,0:T(1,128)S(1)}, u32[]{:S(2)}, u32[]{:S(2)}) collective-permute-start(f32[2,50,1,128]{3,2,1,0:T(1,128)S(1)} %get-tuple-element.235), channel_id=1, source_target_pairs={{1,0},{2,1},{3,2},{4,3},{5,4},{6,5},{7,6},{8,7},{9,8},{10,9},{11,1... | collective-permute-start | bytes 153608 | tf_op jit(solution)/shard_map/ppermute | solution.py:23
  8.8 36.4 %copy-start.1 = (f32[2,50,8,128]{3,2,1,0:T(8,128)S(1)}, f32[2,50,8,128]{3,2,1,0:T(8,128)}, u32[]{:S(2)}) copy-start(f32[2,50,8,128]{3,2,1,0:T(8,128)} %param.17) | copy-start | bytes 1228804
  8.8 36.3 %collective-permute-start.6 = (f32[2,50,1,128]{3,2,1,0:T(1,128)S(1)}, f32[2,50,1,128]{3,2,1,0:T(1,128)S(1)}, u32[]{:S(2)}, u32[]{:S(2)}) collective-permute-start(f32[2,50,1,128]{3,2,1,0:T(1,128)S(1)} %get-tuple-element.234), channel_id=1, source_target_pairs={{0,1},{1,2},{2,3},{3,4},{4,5},{5,6},{6,7},{7,8},{8,9},{9,10},{10,1... | collective-permute-start | bytes 153608 | tf_op jit(solution)/shard_map/ppermute | solution.py:22
  10.1 9.7 %collective-permute-start = (f32[2,50,8,1]{3,2,1,0:T(8,128)S(1)}, f32[2,50,8,1]{3,2,1,0:T(8,128)S(1)}, u32[]{:S(2)}, u32[]{:S(2)}) collective-permute-start(f32[2,50,8,1]{3,2,1,0:T(8,128)S(1)} %get-tuple-element.233), channel_id=1, source_target_pairs={{16,0},{32,16},{48,32},{64,48},{80,64},{96,80},{112,96},{17,1},{33... | collective-permute-start | bytes 9608 | tf_op jit(solution)/shard_map/ppermute | solution.py:23
  13.1 32.0 %collective-permute-start.5 = (f32[2,50,1,128]{3,2,1,0:T(1,128)S(1)}, f32[2,50,1,128]{3,2,1,0:T(1,128)S(1)}, u32[]{:S(2)}, u32[]{:S(2)}) collective-permute-start(f32[2,50,1,128]{3,2,1,0:T(1,128)S(1)} %get-tuple-element.238), channel_id=1, source_target_pairs={{1,0},{2,1},{3,2},{4,3},{5,4},{6,5},{7,6},{8,7},{9,8},{10,9},{11,1... | collective-permute-start | bytes 153608 | tf_op jit(solution)/shard_map/ppermute | solution.py:23
  18.1 27.0 %collective-permute-start.7 = (f32[2,50,1,128]{3,2,1,0:T(1,128)S(1)}, f32[2,50,1,128]{3,2,1,0:T(1,128)S(1)}, u32[]{:S(2)}, u32[]{:S(2)}) collective-permute-start(f32[2,50,1,128]{3,2,1,0:T(1,128)S(1)} %get-tuple-element.239), channel_id=1, source_target_pairs={{0,1},{1,2},{2,3},{3,4},{4,5},{5,6},{6,7},{7,8},{8,9},{9,10},{10,1... | collective-permute-start | bytes 153608 | tf_op jit(solution)/shard_map/ppermute | solution.py:22
  19.8 9.3 %collective-permute-start.1 = (f32[2,50,8,1]{3,2,1,0:T(8,128)S(1)}, f32[2,50,8,1]{3,2,1,0:T(8,128)S(1)}, u32[]{:S(2)}, u32[]{:S(2)}) collective-permute-start(f32[2,50,8,1]{3,2,1,0:T(8,128)S(1)} %get-tuple-element.236), channel_id=1, source_target_pairs={{16,0},{32,16},{48,32},{64,48},{80,64},{96,80},{112,96},{17,1},{33... | collective-permute-start | bytes 9608 | tf_op jit(solution)/shard_map/ppermute | solution.py:23
  29.0 6.8 %collective-permute-start.2 = (f32[2,50,8,1]{3,2,1,0:T(8,128)S(1)}, f32[2,50,8,1]{3,2,1,0:T(8,128)S(1)}, u32[]{:S(2)}, u32[]{:S(2)}) collective-permute-start(f32[2,50,8,1]{3,2,1,0:T(8,128)S(1)} %get-tuple-element.232), channel_id=1, source_target_pairs={{0,16},{16,32},{32,48},{48,64},{64,80},{80,96},{96,112},{1,17},{17... | collective-permute-start | bytes 9608 | tf_op jit(solution)/shard_map/ppermute | solution.py:22
  35.8 9.3 %collective-permute-start.3 = (f32[2,50,8,1]{3,2,1,0:T(8,128)S(1)}, f32[2,50,8,1]{3,2,1,0:T(8,128)S(1)}, u32[]{:S(2)}, u32[]{:S(2)}) collective-permute-start(f32[2,50,8,1]{3,2,1,0:T(8,128)S(1)} %get-tuple-element.237), channel_id=1, source_target_pairs={{0,16},{16,32},{32,48},{48,64},{64,80},{80,96},{96,112},{1,17},{17... | collective-permute-start | bytes 9608 | tf_op jit(solution)/shard_map/ppermute | solution.py:22
  46.0 16.9 %collective-permute-start.10 = (f32[2,50,1,128]{3,2,1,0:T(1,128)S(1)}, f32[2,50,1,128]{3,2,1,0:T(1,128)S(1)}, u32[]{:S(2)}, u32[]{:S(2)}) collective-permute-start(f32[2,50,1,128]{3,2,1,0:T(1,128)S(1)} %get-tuple-element.230), channel_id=1, source_target_pairs={{1,0},{2,1},{3,2},{4,3},{5,4},{6,5},{7,6},{8,7},{9,8},{10,9},{11,1... | collective-permute-start | bytes 153608 | tf_op jit(solution)/shard_map/ppermute | solution.py:23
  51.2 11.7 %collective-permute-start.11 = (f32[2,50,1,128]{3,2,1,0:T(1,128)S(1)}, f32[2,50,1,128]{3,2,1,0:T(1,128)S(1)}, u32[]{:S(2)}, u32[]{:S(2)}) collective-permute-start(f32[2,50,1,128]{3,2,1,0:T(1,128)S(1)} %get-tuple-element.231), channel_id=1, source_target_pairs={{0,1},{1,2},{2,3},{3,4},{4,5},{5,6},{6,7},{7,8},{8,9},{9,10},{10,1... | collective-permute-start | bytes 153608 | tf_op jit(solution)/shard_map/ppermute | solution.py:22
  51.4 10.3 %collective-permute-start.8 = (f32[2,50,8,1]{3,2,1,0:T(8,128)S(1)}, f32[2,50,8,1]{3,2,1,0:T(8,128)S(1)}, u32[]{:S(2)}, u32[]{:S(2)}) collective-permute-start(f32[2,50,8,1]{3,2,1,0:T(8,128)S(1)} %get-tuple-element.228), channel_id=1, source_target_pairs={{16,0},{32,16},{48,32},{64,48},{80,64},{96,80},{112,96},{17,1},{33... | collective-permute-start | bytes 9608 | tf_op jit(solution)/shard_map/ppermute | solution.py:23
  53.4 9.6 %collective-permute-start.9 = (f32[2,50,8,1]{3,2,1,0:T(8,128)S(1)}, f32[2,50,8,1]{3,2,1,0:T(8,128)S(1)}, u32[]{:S(2)}, u32[]{:S(2)}) collective-permute-start(f32[2,50,8,1]{3,2,1,0:T(8,128)S(1)} %get-tuple-element.229), channel_id=1, source_target_pairs={{0,16},{16,32},{32,48},{48,64},{64,80},{80,96},{96,112},{1,17},{17... | collective-permute-start | bytes 9608 | tf_op jit(solution)/shard_map/ppermute | solution.py:22
  63.5 11.7 %copy-start.11 = (s32[128,1]{0,1:T(1,128)S(1)}, s32[128,1]{0,1:T(1,128)}, u32[]{:S(2)}) copy-start(s32[128,1]{0,1:T(1,128)} %param.22) | copy-start | bytes 1540
  63.8 11.6 %collective-permute-start.12 = (f32[2,50,8,1]{3,2,1,0:T(8,128)S(1)}, f32[2,50,8,1]{3,2,1,0:T(8,128)S(1)}, u32[]{:S(2)}, u32[]{:S(2)}) collective-permute-start(f32[2,50,8,1]{3,2,1,0:T(8,128)S(1)} %get-tuple-element.224), channel_id=1, source_target_pairs={{16,0},{32,16},{48,32},{64,48},{80,64},{96,80},{112,96},{17,1},{33... | collective-permute-start | bytes 9608 | tf_op jit(solution)/shard_map/ppermute | solution.py:23
  65.7 9.7 %collective-permute-start.13 = (f32[2,50,8,1]{3,2,1,0:T(8,128)S(1)}, f32[2,50,8,1]{3,2,1,0:T(8,128)S(1)}, u32[]{:S(2)}, u32[]{:S(2)}) collective-permute-start(f32[2,50,8,1]{3,2,1,0:T(8,128)S(1)} %get-tuple-element.225), channel_id=1, source_target_pairs={{0,16},{16,32},{32,48},{48,64},{64,80},{80,96},{96,112},{1,17},{17... | collective-permute-start | bytes 9608 | tf_op jit(solution)/shard_map/ppermute | solution.py:22
  70.1 6.3 %collective-permute-start.14 = (f32[2,50,1,128]{3,2,1,0:T(1,128)S(1)}, f32[2,50,1,128]{3,2,1,0:T(1,128)S(1)}, u32[]{:S(2)}, u32[]{:S(2)}) collective-permute-start(f32[2,50,1,128]{3,2,1,0:T(1,128)S(1)} %get-tuple-element.226), channel_id=1, source_target_pairs={{1,0},{2,1},{3,2},{4,3},{5,4},{6,5},{7,6},{8,7},{9,8},{10,9},{11,1... | collective-permute-start | bytes 153608 | tf_op jit(solution)/shard_map/ppermute | solution.py:23
  75.3 6.3 %collective-permute-start.15 = (f32[2,50,1,128]{3,2,1,0:T(1,128)S(1)}, f32[2,50,1,128]{3,2,1,0:T(1,128)S(1)}, u32[]{:S(2)}, u32[]{:S(2)}) collective-permute-start(f32[2,50,1,128]{3,2,1,0:T(1,128)S(1)} %get-tuple-element.227), channel_id=1, source_target_pairs={{0,1},{1,2},{2,3},{3,4},{4,5},{5,6},{6,7},{7,8},{8,9},{9,10},{10,1... | collective-permute-start | bytes 153608 | tf_op jit(solution)/shard_map/ppermute | solution.py:22
  82.2 9.8 %copy-start.10 = (s32[128,128]{1,0:T(8,128)S(1)}, s32[128,128]{1,0:T(8,128)}, u32[]{:S(2)}) copy-start(s32[128,128]{1,0:T(8,128)} %param.19) | copy-start | bytes 196612
  82.2 13.2 %copy-start.5 = (f32[2,50,8,128]{3,2,1,0:T(8,128)S(1)}, f32[2,50,8,128]{3,2,1,0:T(8,128)}, u32[]{:S(2)}) copy-start(f32[2,50,8,128]{3,2,1,0:T(8,128)} %param.18) | copy-start | bytes 1228804
  82.5 10.0 %collective-permute-start.16 = (f32[2,50,8,1]{3,2,1,0:T(8,128)S(1)}, f32[2,50,8,1]{3,2,1,0:T(8,128)}, u32[]{:S(2)}, u32[]{:S(2)}) collective-permute-start(f32[2,50,8,1]{3,2,1,0:T(8,128)S(1)} %get-tuple-element.220), channel_id=1, source_target_pairs={{16,0},{32,16},{48,32},{64,48},{80,64},{96,80},{112,96},{17,1},{33... | collective-permute-start | bytes 9608 | tf_op jit(solution)/shard_map/ppermute | solution.py:23
  84.4 9.2 %collective-permute-start.17 = (f32[2,50,8,1]{3,2,1,0:T(8,128)S(1)}, f32[2,50,8,1]{3,2,1,0:T(8,128)}, u32[]{:S(2)}, u32[]{:S(2)}) collective-permute-start(f32[2,50,8,1]{3,2,1,0:T(8,128)S(1)} %get-tuple-element.221), channel_id=1, source_target_pairs={{0,16},{16,32},{32,48},{48,64},{64,80},{80,96},{96,112},{1,17},{17... | collective-permute-start | bytes 9608 | tf_op jit(solution)/shard_map/ppermute | solution.py:22
  88.7 4.9 collective-permute-start.18
  88.8 6.6 %collective-permute-start.19 = (f32[2,50,1,128]{3,2,1,0:T(1,128)S(1)}, f32[2,50,1,128]{3,2,1,0:T(1,128)}, u32[]{:S(2)}, u32[]{:S(2)}) collective-permute-start(f32[2,50,1,128]{3,2,1,0:T(1,128)S(1)} %get-tuple-element.223), channel_id=1, source_target_pairs={{0,1},{1,2},{2,3},{3,4},{4,5},{5,6},{6,7},{7,8},{8,9},{9,10},{10,1... | collective-permute-start | bytes 153608 | tf_op jit(solution)/shard_map/ppermute | solution.py:22
  97.3 124.2 %copy-start.7 = (f32[2,128,128]{2,1,0:T(8,128)S(1)}, f32[2,128,128]{2,1,0:T(8,128)}, u32[]{:S(2)}) copy-start(f32[2,128,128]{2,1,0:T(8,128)} %param.21) | copy-start | bytes 393220
  239.5 15.5 %all-to-all-start.1 = ((f32[2,256,128]{2,0,1:T(2,128)}), f32[2,256,128]{2,0,1:T(2,128)S(1)}, u32[]{:S(2)}, u32[]{:S(2)}) async-start(f32[2,256,128]{2,0,1:T(2,128)} %copy.29), calls=%async_computation.1 | async-start | bytes 524288 | tf_op jit(solution)/shard_map/all_to_all | solution.py:176
  405.8 12.2 %collective-permute-start.22 = (f32[2,50,1,128]{3,2,1,0:T(1,128)S(1)}, f32[2,50,1,128]{3,2,1,0:T(1,128)S(1)}, u32[]{:S(2)}, u32[]{:S(2)}) collective-permute-start(f32[2,50,1,128]{3,2,1,0:T(1,128)S(1)} %get-tuple-element.218), channel_id=1, source_target_pairs={{1,0},{2,1},{3,2},{4,3},{5,4},{6,5},{7,6},{8,7},{9,8},{10,9},{11,1... | collective-permute-start | bytes 153608 | tf_op jit(solution)/shard_map/ppermute | solution.py:23
  406.7 11.3 %collective-permute-start.23 = (f32[2,50,1,128]{3,2,1,0:T(1,128)S(1)}, f32[2,50,1,128]{3,2,1,0:T(1,128)S(1)}, u32[]{:S(2)}, u32[]{:S(2)}) collective-permute-start(f32[2,50,1,128]{3,2,1,0:T(1,128)S(1)} %get-tuple-element.219), channel_id=1, source_target_pairs={{0,1},{1,2},{2,3},{3,4},{4,5},{5,6},{6,7},{7,8},{8,9},{9,10},{10,1... | collective-permute-start | bytes 153608 | tf_op jit(solution)/shard_map/ppermute | solution.py:22
  407.5 9.3 %collective-permute-start.20 = (f32[2,50,8,1]{3,2,1,0:T(8,128)S(1)}, f32[2,50,8,1]{3,2,1,0:T(8,128)S(1)}, u32[]{:S(2)}, u32[]{:S(2)}) collective-permute-start(f32[2,50,8,1]{3,2,1,0:T(8,128)S(1)} %get-tuple-element.216), channel_id=1, source_target_pairs={{16,0},{32,16},{48,32},{64,48},{80,64},{96,80},{112,96},{17,1},{33... | collective-permute-start | bytes 9608 | tf_op jit(solution)/shard_map/ppermute | solution.py:23
  410.5 7.5 %collective-permute-start.21 = (f32[2,50,8,1]{3,2,1,0:T(8,128)S(1)}, f32[2,50,8,1]{3,2,1,0:T(8,128)S(1)}, u32[]{:S(2)}, u32[]{:S(2)}) collective-permute-start(f32[2,50,8,1]{3,2,1,0:T(8,128)S(1)} %get-tuple-element.217), channel_id=1, source_target_pairs={{0,16},{16,32},{32,48},{48,64},{64,80},{80,96},{96,112},{1,17},{17... | collective-permute-start | bytes 9608 | tf_op jit(solution)/shard_map/ppermute | solution.py:22
  418.7 15.9 %collective-permute-start.26 = (f32[2,50,1,128]{3,2,1,0:T(1,128)S(1)}, f32[2,50,1,128]{3,2,1,0:T(1,128)S(1)}, u32[]{:S(2)}, u32[]{:S(2)}) collective-permute-start(f32[2,50,1,128]{3,2,1,0:T(1,128)S(1)} %get-tuple-element.214), channel_id=1, source_target_pairs={{1,0},{2,1},{3,2},{4,3},{5,4},{6,5},{7,6},{8,7},{9,8},{10,9},{11,1... | collective-permute-start | bytes 153608 | tf_op jit(solution)/shard_map/ppermute | solution.py:23
  422.9 11.7 %collective-permute-start.27 = (f32[2,50,1,128]{3,2,1,0:T(1,128)S(1)}, f32[2,50,1,128]{3,2,1,0:T(1,128)S(1)}, u32[]{:S(2)}, u32[]{:S(2)}) collective-permute-start(f32[2,50,1,128]{3,2,1,0:T(1,128)S(1)} %get-tuple-element.215), channel_id=1, source_target_pairs={{0,1},{1,2},{2,3},{3,4},{4,5},{5,6},{6,7},{7,8},{8,9},{9,10},{10,1... | collective-permute-start | bytes 153608 | tf_op jit(solution)/shard_map/ppermute | solution.py:22
  423.1 10.3 %collective-permute-start.24 = (f32[2,50,8,1]{3,2,1,0:T(8,128)S(1)}, f32[2,50,8,1]{3,2,1,0:T(8,128)S(1)}, u32[]{:S(2)}, u32[]{:S(2)}) collective-permute-start(f32[2,50,8,1]{3,2,1,0:T(8,128)S(1)} %get-tuple-element.212), channel_id=1, source_target_pairs={{16,0},{32,16},{48,32},{64,48},{80,64},{96,80},{112,96},{17,1},{33... | collective-permute-start | bytes 9608 | tf_op jit(solution)/shard_map/ppermute | solution.py:23
  425.0 9.6 %collective-permute-start.25 = (f32[2,50,8,1]{3,2,1,0:T(8,128)S(1)}, f32[2,50,8,1]{3,2,1,0:T(8,128)S(1)}, u32[]{:S(2)}, u32[]{:S(2)}) collective-permute-start(f32[2,50,8,1]{3,2,1,0:T(8,128)S(1)} %get-tuple-element.213), channel_id=1, source_target_pairs={{0,16},{16,32},{32,48},{48,64},{64,80},{80,96},{96,112},{1,17},{17... | collective-permute-start | bytes 9608 | tf_op jit(solution)/shard_map/ppermute | solution.py:22
  435.2 16.8 %collective-permute-start.30 = (f32[2,50,1,128]{3,2,1,0:T(1,128)S(1)}, f32[2,50,1,128]{3,2,1,0:T(1,128)S(1)}, u32[]{:S(2)}, u32[]{:S(2)}) collective-permute-start(f32[2,50,1,128]{3,2,1,0:T(1,128)S(1)} %get-tuple-element.210), channel_id=1, source_target_pairs={{1,0},{2,1},{3,2},{4,3},{5,4},{6,5},{7,6},{8,7},{9,8},{10,9},{11,1... | collective-permute-start | bytes 153608 | tf_op jit(solution)/shard_map/ppermute | solution.py:23
  440.4 11.7 %collective-permute-start.31 = (f32[2,50,1,128]{3,2,1,0:T(1,128)S(1)}, f32[2,50,1,128]{3,2,1,0:T(1,128)S(1)}, u32[]{:S(2)}, u32[]{:S(2)}) collective-permute-start(f32[2,50,1,128]{3,2,1,0:T(1,128)S(1)} %get-tuple-element.211), channel_id=1, source_target_pairs={{0,1},{1,2},{2,3},{3,4},{4,5},{5,6},{6,7},{7,8},{8,9},{9,10},{10,1... | collective-permute-start | bytes 153608 | tf_op jit(solution)/shard_map/ppermute | solution.py:22
  440.5 10.3 %collective-permute-start.28 = (f32[2,50,8,1]{3,2,1,0:T(8,128)S(1)}, f32[2,50,8,1]{3,2,1,0:T(8,128)S(1)}, u32[]{:S(2)}, u32[]{:S(2)}) collective-permute-start(f32[2,50,8,1]{3,2,1,0:T(8,128)S(1)} %get-tuple-element.208), channel_id=1, source_target_pairs={{16,0},{32,16},{48,32},{64,48},{80,64},{96,80},{112,96},{17,1},{33... | collective-permute-start | bytes 9608 | tf_op jit(solution)/shard_map/ppermute | solution.py:23
  442.5 9.6 %collective-permute-start.29 = (f32[2,50,8,1]{3,2,1,0:T(8,128)S(1)}, f32[2,50,8,1]{3,2,1,0:T(8,128)S(1)}, u32[]{:S(2)}, u32[]{:S(2)}) collective-permute-start(f32[2,50,8,1]{3,2,1,0:T(8,128)S(1)} %get-tuple-element.209), channel_id=1, source_target_pairs={{0,16},{16,32},{32,48},{48,64},{64,80},{80,96},{96,112},{1,17},{17... | collective-permute-start | bytes 9608 | tf_op jit(solution)/shard_map/ppermute | solution.py:22
  452.6 12.0 %copy-start.6 = (f32[2,50,8,128]{3,2,1,0:T(8,128)S(1)}, f32[2,50,8,128]{3,2,1,0:T(8,128)}, u32[]{:S(2)}) copy-start(f32[2,50,8,128]{3,2,1,0:T(8,128)} %param.15) | copy-start | bytes 1228804
  452.7 18.3 %copy-start.3 = (f32[2,50,8,128]{3,2,1,0:T(8,128)S(1)}, f32[2,50,8,128]{3,2,1,0:T(8,128)}, u32[]{:S(2)}) copy-start(f32[2,50,8,128]{3,2,1,0:T(8,128)} %param.16) | copy-start | bytes 1228804
  452.9 12.4 %collective-permute-start.32 = (f32[2,50,8,1]{3,2,1,0:T(8,128)S(1)}, f32[2,50,8,1]{3,2,1,0:T(8,128)S(1)}, u32[]{:S(2)}, u32[]{:S(2)}) collective-permute-start(f32[2,50,8,1]{3,2,1,0:T(8,128)S(1)} %get-tuple-element.204), channel_id=1, source_target_pairs={{16,0},{32,16},{48,32},{64,48},{80,64},{96,80},{112,96},{17,1},{33... | collective-permute-start | bytes 9608 | tf_op jit(solution)/shard_map/ppermute | solution.py:23
  455.1 10.2 %collective-permute-start.33 = (f32[2,50,8,1]{3,2,1,0:T(8,128)S(1)}, f32[2,50,8,1]{3,2,1,0:T(8,128)S(1)}, u32[]{:S(2)}, u32[]{:S(2)}) collective-permute-start(f32[2,50,8,1]{3,2,1,0:T(8,128)S(1)} %get-tuple-element.205), channel_id=1, source_target_pairs={{0,16},{16,32},{32,48},{48,64},{64,80},{80,96},{96,112},{1,17},{17... | collective-permute-start | bytes 9608 | tf_op jit(solution)/shard_map/ppermute | solution.py:22
  459.5 6.3 %collective-permute-start.34 = (f32[2,50,1,128]{3,2,1,0:T(1,128)S(1)}, f32[2,50,1,128]{3,2,1,0:T(1,128)S(1)}, u32[]{:S(2)}, u32[]{:S(2)}) collective-permute-start(f32[2,50,1,128]{3,2,1,0:T(1,128)S(1)} %get-tuple-element.206), channel_id=1, source_target_pairs={{1,0},{2,1},{3,2},{4,3},{5,4},{6,5},{7,6},{8,7},{9,8},{10,9},{11,1... | collective-permute-start | bytes 153608 | tf_op jit(solution)/shard_map/ppermute | solution.py:23
  464.6 6.3 %collective-permute-start.35 = (f32[2,50,1,128]{3,2,1,0:T(1,128)S(1)}, f32[2,50,1,128]{3,2,1,0:T(1,128)S(1)}, u32[]{:S(2)}, u32[]{:S(2)}) collective-permute-start(f32[2,50,1,128]{3,2,1,0:T(1,128)S(1)} %get-tuple-element.207), channel_id=1, source_target_pairs={{0,1},{1,2},{2,3},{3,4},{4,5},{5,6},{6,7},{7,8},{8,9},{9,10},{10,1... | collective-permute-start | bytes 153608 | tf_op jit(solution)/shard_map/ppermute | solution.py:22
  465.4 136.2 %copy-start.8 = (f32[2,50,8,128]{3,2,1,0:T(8,128)S(1)}, f32[2,50,8,128]{3,2,1,0:T(8,128)}, u32[]{:S(2)}) copy-start(f32[2,50,8,128]{3,2,1,0:T(8,128)} %param.14) | copy-start | bytes 1228804
  536.1 66.4 %copy-start.4 = (f32[2,50,8,128]{3,2,1,0:T(8,128)}, f32[2,50,8,128]{3,2,1,0:T(8,128)S(1)}, u32[]{:S(2)}) copy-start(f32[2,50,8,128]{3,2,1,0:T(8,128)S(1)} %get-tuple-element.186) | copy-start | bytes 1228804
  (1 other events, 5.2 us)
where the time goes:
time: 608 us; the launch traced here: 603 us
  matrix products  218 us (36%)
  blocking collectives  142 us (23%)
  starting transfers between devices  99.3 us (16%)
  waiting for transfers between devices  64.6 us (11%)
  local copies, waits for them, and re-layouts  48.4 us (8%)
  other arithmetic  24.4 us (4%)
    psum x1, blocking collectives, shards(): norm_next = lax.psum(jnp.sum(residual * residual), ('lat', 'lon'))  64.1 us
    psum x1, blocking collectives, shards(): norm_now = lax.psum(jnp.sum(residual * residual), ('lat', 'lon'))  61.9 us
    dot_general x16, matrix products, add_group(): jnp.einsum('vrk,jk->vrj', near_rows[None] * values[:, None, :], near_lat,...  59.1 us
    ppermute x18, starting transfers between devices, with_halo(): after = lax.ppermute(leading, axis, down)  57.2 us
    dot_general x16, matrix products, add_group(): jnp.einsum('vrk,jk->vrj', far_rows[None] * values[:, None, :], far_lat, p...  56.6 us
    dot_general x16, matrix products, one_group(): far_vals = jnp.einsum('vrj,jk->vrk', row_field, far_lat, precision=precise)  55.8 us
    dot_general x16, matrix products, one_group(): jnp.einsum('vrj,jk->vrk', row_field, near_lat, precision=precise)  45.8 us
    ppermute x18, starting transfers between devices, with_halo(): before = lax.ppermute(last, axis, up)  38.1 us
  transfers between devices with their start and end apart: 37, of which 20 were waited for; matrix products, arithmetic and copies ran while one was open for 1% of the time, Pallas kernels for 0%

commit v1 on v0

--- a/solution.py
+++ b/solution.py
@@ -12,49 +12,71 @@
 precise = lax.Precision.HIGHEST
 
 
-def with_halo(value, sides, width, wrap):
-    for axis, dim in sides:
-        size, length = (lax.axis_size(axis), value.shape[dim])
-        up = [(i, (i + 1) % size) for i in range(size if wrap else size - 1)]
-        down = [(j, i) for i, j in up]
-        last = lax.slice_in_dim(value, length - width, length, axis=dim)
-        leading = lax.slice_in_dim(value, 0, width, axis=dim)
-        before = lax.ppermute(last, axis, up)
-        after = lax.ppermute(leading, axis, down)
-        value = jnp.concatenate([before, value, after], axis=dim)
-    return value
-
-
-def rim_lat(field):
-    return with_halo(field, (("lat", 3),), 1, False)
-
-
-def rim_lon(field):
-    return with_halo(field, (("lon", 2),), 1, True)
-
-
-def face_coeffs(diffusivity):
-    lat_wide = rim_lat(diffusivity)
-    lon_wide = rim_lon(diffusivity)
+def neighbour_pairs(lat_devices, lon_devices, lat_step, lon_step):
+    pairs = []
+    for a in range(lat_devices):
+        if not 0 <= a + lat_step < lat_devices:
+            continue
+        for b in range(lon_devices):
+            target = (a + lat_step) * lon_devices + (b + lon_step) % lon_devices
+            pairs.append((a * lon_devices + b, target))
+    return pairs
+
+
+def widen_halo(value, width):
+    lat_devices = lax.axis_size("lat")
+    lon_devices = lax.axis_size("lon")
+    lon_count, lat_count = value.shape[2], value.shape[3]
+    lon_parts = {-1: value[:, :, lon_count - width :], 0: value, 1: value[:, :, :width]}
+    rows = []
+    for lon_side in (-1, 0, 1):
+        row = []
+        for lat_side in (-1, 0, 1):
+            piece = lon_parts[lon_side]
+            if lat_side == -1:
+                piece = piece[:, :, :, lat_count - width :]
+            elif lat_side == 1:
+                piece = piece[:, :, :, :width]
+            if lon_side or lat_side:
+                pairs = neighbour_pairs(lat_devices, lon_devices, -lat_side, -lon_side)
+                piece = lax.ppermute(piece, ("lat", "lon"), pairs)
+            row.append(piece)
+        rows.append(jnp.concatenate(row, axis=3))
+    return jnp.concatenate(rows, axis=2)
+
+
+def face_coeffs(diffusivity, width):
+    wide = widen_halo(diffusivity, width + 1)
+    lat_count = diffusivity.shape[3]
+    lat_devices = lax.axis_size("lat")
+    first = lax.axis_index("lat") * lat_count - width
+    cells = first + jnp.arange(lat_count + 2 * width, dtype=jnp.int32)
+    inside = ((cells >= 0) & (cells < lat_devices * lat_count)).astype(jnp.float32)
+    centre = wide[:, :, 1:-1, 1:-1]
     return (
-        0.5 * (diffusivity + lat_wide[:, :, :, 2:]),
-        0.5 * (diffusivity + lat_wide[:, :, :, :-2]),
-        0.5 * (diffusivity + lon_wide[:, :, 2:, :]),
-        0.5 * (diffusivity + lon_wide[:, :, :-2, :]),
+        inside * (0.5 * (centre + wide[:, :, 1:-1, 2:])),
+        inside * (0.5 * (centre + wide[:, :, 1:-1, :-2])),
+        inside * (0.5 * (centre + wide[:, :, 2:, 1:-1])),
+        inside * (0.5 * (centre + wide[:, :, :-2, 1:-1])),
     )
 
 
 def diffuse(field, coeffs):
-    north_face, south_face, east_face, west_face = coeffs
+    field = widen_halo(field, STEPS)
     for sweep in range(STEPS):
-        lat_wide = rim_lat(field)
-        lon_wide = rim_lon(field)
+        lon_end = field.shape[2] - 1
+        lat_end = field.shape[3] - 1
+        here = field[:, :, 1:lon_end, 1:lat_end]
+        edge = sweep + 1
+        north_face, south_face, east_face, west_face = (
+            c[:, :, edge : c.shape[2] - edge, edge : c.shape[3] - edge] for c in coeffs
+        )
         field = (
-            field
-            + north_face * (lat_wide[:, :, :, 2:] - field)
-            + south_face * (lat_wide[:, :, :, :-2] - field)
-            + east_face * (lon_wide[:, :, 2:, :] - field)
-            + west_face * (lon_wide[:, :, :-2, :] - field)
+            here
+            + north_face * (field[:, :, 1:lon_end, 2:] - here)
+            + south_face * (field[:, :, 1:lon_end, : lat_end - 1] - here)
+            + east_face * (field[:, :, 2:, 1:lat_end] - here)
+            + west_face * (field[:, :, : lon_end - 1, 1:lat_end] - here)
         )
     return field
 
@@ -159,7 +181,7 @@
     lat_devices = lax.axis_size("lat")
     lon_devices = lax.axis_size("lon")
     tile_count = lat_devices * lon_devices
-    coeffs = face_coeffs(diffusivity)
+    coeffs = face_coeffs(diffusivity, STEPS)
 
     def apply_diffusion(field):
         return diffuse(field, coeffs)
@@ -169,7 +191,6 @@
         jnp.float32
     )
     field_shape = direction.shape
-    norm_now = lax.psum(jnp.sum(residual * residual), ("lat", "lon"))
     state_field = deviation * apply_diffusion(direction)
     observed = observe(state_field, stencil, bilinear, obs_weight)
     buffer = jnp.einsum("vbk,bs->vsk", observed, slot_table, precision=precise)
@@ -186,11 +207,22 @@
     weighted = obs_weight * jnp.einsum("vsk,bs->vbk", returned, slot_table, precision=precise)
     spread_field = deviation * spread_back(weighted, stencil, bilinear, field_shape)
     image_field = direction + apply_diffusion(spread_field)
-    curvature = lax.psum(jnp.sum(direction * image_field), ("lat", "lon"))
+    sums = lax.psum(
+        jnp.stack(
+            [
+                jnp.sum(residual * residual),
+                jnp.sum(direction * image_field),
+                jnp.sum(residual * image_field),
+                jnp.sum(image_field * image_field),
+            ]
+        ),
+        ("lat", "lon"),
+    )
+    norm_now, curvature, cross, image_norm = sums[0], sums[1], sums[2], sums[3]
     step_size = norm_now / curvature
     increment = increment + step_size * direction
     residual = residual - step_size * image_field
-    norm_next = lax.psum(jnp.sum(residual * residual), ("lat", "lon"))
+    norm_next = norm_now - 2.0 * step_size * cross + step_size * step_size * image_norm
     direction = residual + norm_next / norm_now * direction
     return (increment, residual, direction)
 

time: 608 us -> 609 us (level)
  blocking collectives: 142 us -> 85.8 us
  other arithmetic: 24.4 us -> 74.7 us
  matrix products: 218 us -> 245 us
  local copies, waits for them, and re-layouts: 48.4 us -> 75.1 us
  waiting for transfers between devices: 64.6 us -> 38.7 us
  starting transfers between devices: 99.3 us -> 73.6 us
    psum x2 -> x1, blocking collectives: 126 us -> 66.4 us  [shards(): lax.psum(jnp.stack([jnp.sum(residual * residual), jnp.sum(direction * ima...]
    ppermute x36 -> x24, starting transfers between devices: 95.3 us -> 68.7 us  [widen_halo(): piece = lax.ppermute(piece, ('lat', 'lon'), pairs)]
    ppermute x36 -> x24, waiting for transfers between devices: 53.1 us -> 27.5 us  [widen_halo(): piece = lax.ppermute(piece, ('lat', 'lon'), pairs)]
    convert_element_type x32, other arithmetic: 9.42 us -> 28.7 us  [block_maps(): near_rows = (rows == row_base[None, :]).astype(jnp.float32)]
    add x6, other arithmetic: 3.84 us -> 21.8 us  [diffuse(): here + north_face * (field[:, :, 1:lon_end, 2:] - here)]
    dot_general x16, matrix products: 45.8 us -> 61.9 us  [one_group(): jnp.einsum('vrj,jk->vrk', row_field, near_lat, precision=precise)]
    while x0 -> x32, local copies, waits for them, and re-layouts: none -> 9.43 us
    dynamic_update_slice x16, local copies, waits for them, and re-layouts: 0.21 us -> 9.6 us  [observe(): values = lax.map(one_group, (bases, corner_weights))]
  transfers between devices with their start and end apart: 37 -> 25, of which waited for: 20 -> 6; matrix products, arithmetic and copies ran while one was open for 1% -> 2% of each run, Pallas kernels for 0% -> 0%
where the time goes in v1:
time: 609 us; the launch traced here: 600 us
  matrix products  245 us (40%)
  blocking collectives  85.8 us (14%)
  local copies, waits for them, and re-layouts  75.1 us (12%)
  other arithmetic  74.7 us (12%)
  starting transfers between devices  73.6 us (12%)
  waiting for transfers between devices  38.7 us (6%)
    ppermute x24, starting transfers between devices, widen_halo(): piece = lax.ppermute(piece, ('lat', 'lon'), pairs)  68.7 us
    dot_general x16, matrix products, add_group(): jnp.einsum('vrk,jk->vrj', near_rows[None] * values[:, None, :], near_lat,...  67.8 us
    psum x1, blocking collectives, shards(): lax.psum(jnp.stack([jnp.sum(residual * residual), jnp.sum(direction * ima...  66.4 us
    dot_general x16, matrix products, one_group(): jnp.einsum('vrj,jk->vrk', row_field, near_lat, precision=precise)  61.9 us
    dot_general x16, matrix products, add_group(): jnp.einsum('vrk,jk->vrj', far_rows[None] * values[:, None, :], far_lat, p...  56.7 us
    dot_general x16, matrix products, one_group(): far_vals = jnp.einsum('vrj,jk->vrk', row_field, far_lat, precision=precise)  55.3 us
    convert_element_type x32, other arithmetic, block_maps(): near_rows = (rows == row_base[None, :]).astype(jnp.float32)  28.7 us
    slice x32, local copies, waits for them, and re-layouts, block_maps(): far_lat = lat_weights(lat_base, weights_four[2], weights_four[3], lat_count)  28.4 us
  transfers between devices with their start and end apart: 25, of which 6 were waited for; matrix products, arithmetic and copies ran while one was open for 2% of the time, Pallas kernels for 0%

profile of v1, /device:TPU:1, one launch (start us, length us, event | category | flops | bytes accessed | tf_op | source)
XLA Modules:
  0.0 599.6 jit_solution(13231982792486552952)
XLA Ops:
  3.3 4.6 collective-permute-start.10
  14.5 7.3 %collective-permute-start.5 = (f32[2,50,4,4]{3,2,1,0:T(4,128)S(1)}, f32[2,50,4,4]{3,2,1,0:T(4,128)S(1)}, u32[]{:S(2)}, u32[]{:S(2)}) collective-permute-start(f32[2,50,4,4]{3,2,1,0:T(4,128)S(1)} %get-tuple-element.223), channel_id=1, source_target_pairs={{0,31},{1,16},{2,17},{3,18},{4,19},{5,20},{6,21},{7,22},{8,23},{9,... | collective-permute-start | bytes 19208 | tf_op jit(solution)/shard_map/ppermute | solution.py:42
  28.4 5.1 collective-permute-start.13
  35.5 4.4 collective-permute-start.3
  40.5 4.4 collective-permute-start.6
  45.5 6.0 collective-permute-done.15
  55.4 7.9 %collective-permute-done.4 = f32[2,50,8,4]{3,2,1,0:T(8,128)} collective-permute-done((f32[2,50,8,4]{3,2,1,0:T(8,128)}, f32[2,50,8,4]{3,2,1,0:T(8,128)}, u32[]{:S(2)}, u32[]{:S(2)}) %collective-permute-start.4) | collective-permute-done | bytes 12832 | tf_op jit(solution)/shard_map/ppermute | solution.py:42
  73.4 5.8 collective-permute-done.8
  96.7 158.3 %while.25 = (s32[]{:T(128)}, f32[16,2,1024]{2,1,0:T(2,128)}, s32[16,1024]{1,0:T(8,128)S(1)}, f32[16,4,1024]{2,1,0:T(4,128)}, f32[2,400,128]{2,1,0:T(8,128)}, /*index=5*/s32[]{:T(128)}, s32[]{:T(128)}, s32[]{}, s32[]{}, s32[]{}) while((s32[]{:T(128)}, f32[16,2,1024]{2,1,0:T(2,128)}, s32[16,1024]{1,0:T(8,128)S(1)}, f32[16,4,1024]{2,1,0:T(4,128)}, ...), condition=%wide.region_4.5_spmd, body=%wide.region_2.4_spmd.sunk | while | flops 2522825728 | bytes 15692477 | solution.py:123
  97.6 3.9 fusion.178
  107.5 3.9 fusion.178
  117.4 3.9 fusion.178
  127.3 3.9 fusion.178
  137.2 3.9 fusion.178
  147.1 3.9 fusion.178
  157.0 3.9 fusion.178
  166.9 3.9 fusion.178
  176.8 3.9 fusion.178
  186.7 3.9 fusion.178
  196.6 3.9 fusion.178
  216.4 3.9 fusion.178
  226.3 3.9 fusion.178
  236.2 3.9 fusion.178
  246.0 3.9 fusion.178
  259.7 19.4 %all_to_all.10 = f32[2,256,128]{2,0,1:T(2,128)S(1)} all-to-all(f32[2,256,128]{2,0,1:T(2,128)S(1)} %copy.27), channel_id=1, replica_groups=mesh['lat'=8,'lon'=16] {'lat','lon'}, dimensions={1} | all-to-all | bytes 524288 | tf_op jit(solution)/shard_map/all_to_all | solution.py:199
  280.4 4.9 all-to-all-start.1
  285.3 11.2 %all-to-all-done.1 = f32[2,256,128]{2,0,1:T(2,128)} async-done(((f32[2,256,128]{2,0,1:T(2,128)}), f32[2,256,128]{2,0,1:T(2,128)}, u32[]{:S(2)}, u32[]{:S(2)}) %all-to-all-start.1) | async-done | bytes 262176 | tf_op jit(solution)/shard_map/all_to_all | solution.py:197
  300.1 176.3 %while.26 = (s32[]{:T(128)}, f32[2,400,128]{2,1,0:T(8,128)}, s32[16,1024]{1,0:T(8,128)S(1)}, f32[16,2,1024]{2,1,0:T(2,128)}, f32[16,4,1024]{2,1,0:T(4,128)}, /*index=5*/s32[]{:T(128)}, s32[]{:T(128)}, s32[]{}, s32[]{}, s32[]{}) while((s32[]{:T(128)}, f32[2,400,128]{2,1,0:T(8,128)}, s32[16,1024]{1,0:T(8,128)S(1)}, ...), condition=%wide.region_6.7_spmd.clone, body=%wide.region_5.6_spmd.clone.sunk | while | flops 2521496576 | bytes 8327343 | solution.py:148
  303.2 4.2 fusion.186
  314.1 4.2 fusion.186
  325.1 4.2 fusion.186
  336.2 4.2 fusion.186
  347.2 4.2 fusion.186
  358.2 4.2 fusion.186
  369.3 4.2 fusion.186
  380.3 4.2 fusion.186
  391.3 4.2 fusion.186
  402.3 4.2 fusion.186
  413.3 4.2 fusion.186
  424.4 4.2 fusion.186
  435.4 4.2 fusion.186
  446.4 4.2 fusion.186
  457.4 4.2 fusion.186
  468.5 4.2 fusion.186
  483.6 3.9 collective-permute-start.22
  487.6 5.1 collective-permute-start.21
  501.9 7.1 %collective-permute-done.23 = f32[2,50,4,4]{3,2,1,0:T(4,128)S(1)} collective-permute-done((f32[2,50,4,4]{3,2,1,0:T(4,128)S(1)}, f32[2,50,4,4]{3,2,1,0:T(4,128)S(1)}, u32[]{:S(2)}, u32[]{:S(2)}) %collective-permute-start.23) | collective-permute-done | bytes 6432 | tf_op jit(solution)/shard_map/ppermute | solution.py:42
  526.1 66.4 %psum.7 = f32[4]{0:T(128)S(1)} all-reduce(f32[4]{0:T(128)S(1)} %pad_maximum_fusion), channel_id=1, replica_groups=mesh['lat'=8,'lon'=16] {'lat','lon'}, use_global_device_ids=true, to_apply=%region_10.11 | all-reduce | flops 4 | bytes 32 | tf_op jit(solution)/shard_map/psum | solution.py:210
  (356 shorter events, 303.9 us)
Async XLA Ops:
  0.6 278.5 %copy-start = (f32[128,128]{1,0:T(8,128)S(1)}, f32[128,128]{1,0:T(8,128)}, u32[]{:S(2)}) copy-start(f32[128,128]{1,0:T(8,128)} %param.23) | copy-start | bytes 196612
  0.6 7.3 %copy-start.7 = (f32[2,50,8,128]{3,2,1,0:T(8,128)S(1)}, f32[2,50,8,128]{3,2,1,0:T(8,128)}, u32[]{:S(2)}) copy-start(f32[2,50,8,128]{3,2,1,0:T(8,128)} %param.16) | copy-start | bytes 1228804
  3.3 20.4 %copy-start.6 = (f32[2,50,8,128]{3,2,1,0:T(8,128)S(1)}, f32[2,50,8,128]{3,2,1,0:T(8,128)}, u32[]{:S(2)}) copy-start(f32[2,50,8,128]{3,2,1,0:T(8,128)} %param.17) | copy-start | bytes 1228804
  3.3 37.1 %collective-permute-start.10 = (f32[2,50,5,5]{3,2,1,0:T(8,128)S(1)}, f32[2,50,5,5]{3,2,1,0:T(8,128)S(1)}, u32[]{:S(2)}, u32[]{:S(2)}) collective-permute-start(f32[2,50,5,5]{3,2,1,0:T(8,128)S(1)} %get-tuple-element.215), channel_id=1, source_target_pairs={{16,1},{17,2},{18,3},{19,4},{20,5},{21,6},{22,7},{23,8},{24,9},{25... | collective-permute-start | bytes 30008 | tf_op jit(solution)/shard_map/ppermute | solution.py:42
  8.3 19.4 %collective-permute-start = (f32[2,50,4,4]{3,2,1,0:T(4,128)S(1)}, f32[2,50,4,4]{3,2,1,0:T(4,128)S(1)}, u32[]{:S(2)}, u32[]{:S(2)}) collective-permute-start(f32[2,50,4,4]{3,2,1,0:T(4,128)S(1)} %get-tuple-element.221), channel_id=1, source_target_pairs={{0,17},{1,18},{2,19},{3,20},{4,21},{5,22},{6,23},{7,24},{8,25},{9,... | collective-permute-start | bytes 19208 | tf_op jit(solution)/shard_map/ppermute | solution.py:42
  12.0 21.6 %collective-permute-start.2 = (f32[2,50,4,4]{3,2,1,0:T(4,128)S(1)}, f32[2,50,4,4]{3,2,1,0:T(4,128)S(1)}, u32[]{:S(2)}, u32[]{:S(2)}) collective-permute-start(f32[2,50,4,4]{3,2,1,0:T(4,128)S(1)} %get-tuple-element.224), channel_id=1, source_target_pairs={{16,1},{17,2},{18,3},{19,4},{20,5},{21,6},{22,7},{23,8},{24,9},{25... | collective-permute-start | bytes 19208 | tf_op jit(solution)/shard_map/ppermute | solution.py:42
  14.5 21.0 %collective-permute-start.5 = (f32[2,50,4,4]{3,2,1,0:T(4,128)S(1)}, f32[2,50,4,4]{3,2,1,0:T(4,128)S(1)}, u32[]{:S(2)}, u32[]{:S(2)}) collective-permute-start(f32[2,50,4,4]{3,2,1,0:T(4,128)S(1)} %get-tuple-element.223), channel_id=1, source_target_pairs={{0,31},{1,16},{2,17},{3,18},{4,19},{5,20},{6,21},{7,22},{8,23},{9,... | collective-permute-start | bytes 19208 | tf_op jit(solution)/shard_map/ppermute | solution.py:42
  21.8 18.2 %collective-permute-start.7 = (f32[2,50,4,4]{3,2,1,0:T(4,128)S(1)}, f32[2,50,4,4]{3,2,1,0:T(4,128)S(1)}, u32[]{:S(2)}, u32[]{:S(2)}) collective-permute-start(f32[2,50,4,4]{3,2,1,0:T(4,128)S(1)} %get-tuple-element.222), channel_id=1, source_target_pairs={{16,15},{17,0},{18,1},{19,2},{20,3},{21,4},{22,5},{23,6},{24,7},{2... | collective-permute-start | bytes 19208 | tf_op jit(solution)/shard_map/ppermute | solution.py:42
  25.7 1.8 copy-start.18
  25.7 29.7 %copy-start.16 = (s32[128,128]{1,0:T(8,128)S(1)}, s32[128,128]{1,0:T(8,128)}, u32[]{:S(2)}) copy-start(s32[128,128]{1,0:T(8,128)} %param.19) | copy-start | bytes 196612
  28.4 17.0 %collective-permute-start.13 = (f32[2,50,5,5]{3,2,1,0:T(8,128)}, f32[2,50,5,5]{3,2,1,0:T(8,128)S(1)}, u32[]{:S(2)}, u32[]{:S(2)}) collective-permute-start(f32[2,50,5,5]{3,2,1,0:T(8,128)} %get-tuple-element.214), channel_id=1, source_target_pairs={{0,31},{1,16},{2,17},{3,18},{4,19},{5,20},{6,21},{7,22},{8,23},{9,... | collective-permute-start | bytes 30008 | tf_op jit(solution)/shard_map/ppermute | solution.py:42
  33.6 6.9 %copy-start.13 = (f32[2,50,4,4]{3,2,1,0:T(4,128)}, f32[2,50,4,4]{3,2,1,0:T(4,128)S(1)}, u32[]{:S(2)}) copy-start(f32[2,50,4,4]{3,2,1,0:T(4,128)S(1)} %collective-permute-done.2) | copy-start | bytes 19204
  33.6 17.9 %collective-permute-start.15 = (f32[2,50,5,5]{3,2,1,0:T(8,128)S(1)}, f32[2,50,5,5]{3,2,1,0:T(8,128)S(1)}, u32[]{:S(2)}, u32[]{:S(2)}) collective-permute-start(f32[2,50,5,5]{3,2,1,0:T(8,128)S(1)} %get-tuple-element.216), channel_id=1, source_target_pairs={{16,15},{17,0},{18,1},{19,2},{20,3},{21,4},{22,5},{23,6},{24,7},{2... | collective-permute-start | bytes 30008 | tf_op jit(solution)/shard_map/ppermute | solution.py:42
  35.5 4.9 copy-start.14
  35.5 15.9 %collective-permute-start.3 = (f32[2,50,8,4]{3,2,1,0:T(8,128)}, f32[2,50,8,4]{3,2,1,0:T(8,128)}, u32[]{:S(2)}, u32[]{:S(2)}) collective-permute-start(f32[2,50,8,4]{3,2,1,0:T(8,128)} %get-tuple-element.227), channel_id=1, source_target_pairs={{0,16},{1,17},{2,18},{3,19},{4,20},{5,21},{6,22},{7,23},{8,24},{9,... | collective-permute-start | bytes 38408 | tf_op jit(solution)/shard_map/ppermute | solution.py:42
  40.0 4.9 copy-start.15
  40.0 25.2 %collective-permute-start.1 = (f32[2,50,4,128]{3,2,1,0:T(4,128)}, f32[2,50,4,128]{3,2,1,0:T(4,128)}, u32[]{:S(2)}, u32[]{:S(2)}) collective-permute-start(f32[2,50,4,128]{3,2,1,0:T(4,128)} %get-tuple-element.225), channel_id=1, source_target_pairs={{0,1},{1,2},{2,3},{3,4},{4,5},{5,6},{6,7},{7,8},{8,9},{9,10},{10,1... | collective-permute-start | bytes 614408 | tf_op jit(solution)/shard_map/ppermute | solution.py:42
  40.5 28.0 %collective-permute-start.6 = (f32[2,50,4,128]{3,2,1,0:T(4,128)}, f32[2,50,4,128]{3,2,1,0:T(4,128)}, u32[]{:S(2)}, u32[]{:S(2)}) collective-permute-start(f32[2,50,4,128]{3,2,1,0:T(4,128)} %get-tuple-element.226), channel_id=1, source_target_pairs={{0,15},{1,0},{2,1},{3,2},{4,3},{5,4},{6,5},{7,6},{8,7},{9,8},{10,9... | collective-permute-start | bytes 614408 | tf_op jit(solution)/shard_map/ppermute | solution.py:42
  45.5 33.8 %collective-permute-start.14 = (f32[2,50,5,128]{3,2,1,0:T(8,128)}, f32[2,50,5,128]{3,2,1,0:T(8,128)}, u32[]{:S(2)}, u32[]{:S(2)}) collective-permute-start(f32[2,50,5,128]{3,2,1,0:T(8,128)} %get-tuple-element.218), channel_id=1, source_target_pairs={{0,15},{1,0},{2,1},{3,2},{4,3},{5,4},{6,5},{7,6},{8,7},{9,8},{10,9... | collective-permute-start | bytes 768008 | tf_op jit(solution)/shard_map/ppermute | solution.py:42
  51.5 27.8 %collective-permute-start.9 = (f32[2,50,5,128]{3,2,1,0:T(8,128)}, f32[2,50,5,128]{3,2,1,0:T(8,128)S(1)}, u32[]{:S(2)}, u32[]{:S(2)}) collective-permute-start(f32[2,50,5,128]{3,2,1,0:T(8,128)} %get-tuple-element.217), channel_id=1, source_target_pairs={{0,1},{1,2},{2,3},{3,4},{4,5},{5,6},{6,7},{7,8},{8,9},{9,10},{10,1... | collective-permute-start | bytes 768008 | tf_op jit(solution)/shard_map/ppermute | solution.py:42
  51.5 11.8 %collective-permute-start.4 = (f32[2,50,8,4]{3,2,1,0:T(8,128)}, f32[2,50,8,4]{3,2,1,0:T(8,128)}, u32[]{:S(2)}, u32[]{:S(2)}) collective-permute-start(f32[2,50,8,4]{3,2,1,0:T(8,128)} %get-tuple-element.228), channel_id=1, source_target_pairs={{16,0},{17,1},{18,2},{19,3},{20,4},{21,5},{22,6},{23,7},{24,8},{25... | collective-permute-start | bytes 38408 | tf_op jit(solution)/shard_map/ppermute | solution.py:42
  63.3 15.9 %collective-permute-start.8 = (f32[2,50,5,5]{3,2,1,0:T(8,128)S(1)}, f32[2,50,5,5]{3,2,1,0:T(8,128)S(1)}, u32[]{:S(2)}, u32[]{:S(2)}) collective-permute-start(f32[2,50,5,5]{3,2,1,0:T(8,128)S(1)} %get-tuple-element.213), channel_id=1, source_target_pairs={{0,17},{1,18},{2,19},{3,20},{4,21},{5,22},{6,23},{7,24},{8,25},{9,... | collective-permute-start | bytes 30008 | tf_op jit(solution)/shard_map/ppermute | solution.py:42
  65.2 14.0 %collective-permute-start.11 = (f32[2,50,8,5]{3,2,1,0:T(8,128)}, f32[2,50,8,5]{3,2,1,0:T(8,128)S(1)}, u32[]{:S(2)}, u32[]{:S(2)}) collective-permute-start(f32[2,50,8,5]{3,2,1,0:T(8,128)} %get-tuple-element.219), channel_id=1, source_target_pairs={{0,16},{1,17},{2,18},{3,19},{4,20},{5,21},{6,22},{7,23},{8,24},{9,... | collective-permute-start | bytes 48008 | tf_op jit(solution)/shard_map/ppermute | solution.py:42
  68.4 10.8 %collective-permute-start.12 = (f32[2,50,8,5]{3,2,1,0:T(8,128)}, f32[2,50,8,5]{3,2,1,0:T(8,128)S(1)}, u32[]{:S(2)}, u32[]{:S(2)}) collective-permute-start(f32[2,50,8,5]{3,2,1,0:T(8,128)} %get-tuple-element.220), channel_id=1, source_target_pairs={{16,0},{17,1},{18,2},{19,3},{20,4},{21,5},{22,6},{23,7},{24,8},{25... | collective-permute-start | bytes 48008 | tf_op jit(solution)/shard_map/ppermute | solution.py:42
  83.7 11.2 %copy-start.1 = (f32[2,50,16,136]{3,2,1,0:T(8,128)}, f32[2,50,16,136]{3,2,1,0:T(8,128)S(1)}, u32[]{:S(2)}) copy-start(f32[2,50,16,136]{3,2,1,0:T(8,128)S(1)} %get-tuple-element.202) | copy-start | bytes 2611204
  83.7 11.2 %copy-start.3 = (f32[2,50,16,136]{3,2,1,0:T(8,128)}, f32[2,50,16,136]{3,2,1,0:T(8,128)S(1)}, u32[]{:S(2)}) copy-start(f32[2,50,16,136]{3,2,1,0:T(8,128)S(1)} %get-tuple-element.203) | copy-start | bytes 2611204
  91.0 3.9 copy-start.9
  96.7 161.5 %copy-start.11 = (f32[2,128,128]{2,1,0:T(8,128)S(1)}, f32[2,128,128]{2,1,0:T(8,128)}, u32[]{:S(2)}) copy-start(f32[2,128,128]{2,1,0:T(8,128)} %param.21) | copy-start | bytes 393220
  101.5 1.0 copy-start.5
  111.4 1.0 copy-start.5
  121.3 1.0 copy-start.5
  141.1 1.0 copy-start.5
  151.0 1.0 copy-start.5
  160.9 1.0 copy-start.5
  258.2 38.4 %copy-start.17 = (s32[128]{0:T(128)S(1)}, s32[128]{0:T(128)}, u32[]{:S(2)}) copy-start(s32[128]{0:T(128)} %fusion.145) | copy-start | bytes 1540
  280.4 16.2 %all-to-all-start.1 = ((f32[2,256,128]{2,0,1:T(2,128)}), f32[2,256,128]{2,0,1:T(2,128)}, u32[]{:S(2)}, u32[]{:S(2)}) async-start(f32[2,256,128]{2,0,1:T(2,128)} %copy.29), calls=%async_computation.1 | async-start | bytes 524288 | tf_op jit(solution)/shard_map/all_to_all | solution.py:197
  478.0 14.8 %collective-permute-start.16 = (f32[2,50,4,4]{3,2,1,0:T(4,128)S(1)}, f32[2,50,4,4]{3,2,1,0:T(4,128)S(1)}, u32[]{:S(2)}, u32[]{:S(2)}) collective-permute-start(f32[2,50,4,4]{3,2,1,0:T(4,128)S(1)} %get-tuple-element.205), channel_id=1, source_target_pairs={{0,17},{1,18},{2,19},{3,20},{4,21},{5,22},{6,23},{7,24},{8,25},{9,... | collective-permute-start | bytes 19208 | tf_op jit(solution)/shard_map/ppermute | solution.py:42
  480.7 15.9 %collective-permute-start.18 = (f32[2,50,4,4]{3,2,1,0:T(4,128)S(1)}, f32[2,50,4,4]{3,2,1,0:T(4,128)S(1)}, u32[]{:S(2)}, u32[]{:S(2)}) collective-permute-start(f32[2,50,4,4]{3,2,1,0:T(4,128)S(1)} %get-tuple-element.208), channel_id=1, source_target_pairs={{16,1},{17,2},{18,3},{19,4},{20,5},{21,6},{22,7},{23,8},{24,9},{25... | collective-permute-start | bytes 19208 | tf_op jit(solution)/shard_map/ppermute | solution.py:42
  482.6 26.4 %collective-permute-start.17 = (f32[2,50,4,128]{3,2,1,0:T(4,128)S(1)}, f32[2,50,4,128]{3,2,1,0:T(4,128)S(1)}, u32[]{:S(2)}, u32[]{:S(2)}) collective-permute-start(f32[2,50,4,128]{3,2,1,0:T(4,128)S(1)} %get-tuple-element.209), channel_id=1, source_target_pairs={{0,1},{1,2},{2,3},{3,4},{4,5},{5,6},{6,7},{7,8},{8,9},{9,10},{10,1... | collective-permute-start | bytes 614408 | tf_op jit(solution)/shard_map/ppermute | solution.py:42
  483.6 25.4 %collective-permute-start.22 = (f32[2,50,4,128]{3,2,1,0:T(4,128)S(1)}, f32[2,50,4,128]{3,2,1,0:T(4,128)S(1)}, u32[]{:S(2)}, u32[]{:S(2)}) collective-permute-start(f32[2,50,4,128]{3,2,1,0:T(4,128)S(1)} %get-tuple-element.210), channel_id=1, source_target_pairs={{0,15},{1,0},{2,1},{3,2},{4,3},{5,4},{6,5},{7,6},{8,7},{9,8},{10,9... | collective-permute-start | bytes 614408 | tf_op jit(solution)/shard_map/ppermute | solution.py:42
  487.6 11.8 %collective-permute-start.21 = (f32[2,50,4,4]{3,2,1,0:T(4,128)S(1)}, f32[2,50,4,4]{3,2,1,0:T(4,128)S(1)}, u32[]{:S(2)}, u32[]{:S(2)}) collective-permute-start(f32[2,50,4,4]{3,2,1,0:T(4,128)S(1)} %get-tuple-element.207), channel_id=1, source_target_pairs={{0,31},{1,16},{2,17},{3,18},{4,19},{5,20},{6,21},{7,22},{8,23},{9,... | collective-permute-start | bytes 19208 | tf_op jit(solution)/shard_map/ppermute | solution.py:42
  492.8 16.2 %collective-permute-start.19 = (f32[2,50,8,4]{3,2,1,0:T(8,128)S(1)}, f32[2,50,8,4]{3,2,1,0:T(8,128)S(1)}, u32[]{:S(2)}, u32[]{:S(2)}) collective-permute-start(f32[2,50,8,4]{3,2,1,0:T(8,128)S(1)} %get-tuple-element.211), channel_id=1, source_target_pairs={{0,16},{1,17},{2,18},{3,19},{4,20},{5,21},{6,22},{7,23},{8,24},{9,... | collective-permute-start | bytes 38408 | tf_op jit(solution)/shard_map/ppermute | solution.py:42
  496.6 12.4 %collective-permute-start.20 = (f32[2,50,8,4]{3,2,1,0:T(8,128)S(1)}, f32[2,50,8,4]{3,2,1,0:T(8,128)S(1)}, u32[]{:S(2)}, u32[]{:S(2)}) collective-permute-start(f32[2,50,8,4]{3,2,1,0:T(8,128)S(1)} %get-tuple-element.212), channel_id=1, source_target_pairs={{16,0},{17,1},{18,2},{19,3},{20,4},{21,5},{22,6},{23,7},{24,8},{25... | collective-permute-start | bytes 38408 | tf_op jit(solution)/shard_map/ppermute | solution.py:42
  499.5 10.9 %copy-start.2 = (f32[2,50,16,136]{3,2,1,0:T(8,128)S(1)}, f32[2,50,16,136]{3,2,1,0:T(8,128)}, u32[]{:S(2)}) copy-start(f32[2,50,16,136]{3,2,1,0:T(8,128)} %copy-done.1) | copy-start | bytes 2611204
  499.5 10.9 %copy-start.4 = (f32[2,50,16,136]{3,2,1,0:T(8,128)S(1)}, f32[2,50,16,136]{3,2,1,0:T(8,128)}, u32[]{:S(2)}) copy-start(f32[2,50,16,136]{3,2,1,0:T(8,128)} %copy-done.3) | copy-start | bytes 2611204
  499.5 9.4 %collective-permute-start.23 = (f32[2,50,4,4]{3,2,1,0:T(4,128)S(1)}, f32[2,50,4,4]{3,2,1,0:T(4,128)S(1)}, u32[]{:S(2)}, u32[]{:S(2)}) collective-permute-start(f32[2,50,4,4]{3,2,1,0:T(4,128)S(1)} %get-tuple-element.206), channel_id=1, source_target_pairs={{16,15},{17,0},{18,1},{19,2},{20,3},{21,4},{22,5},{23,6},{24,7},{2... | collective-permute-start | bytes 19208 | tf_op jit(solution)/shard_map/ppermute | solution.py:42
  517.5 3.6 copy-start.8
  517.5 3.6 copy-start.10
  (11 other events, 10.7 us)

commit v2 on v1

v2 whole, which is shorter than its diff:
```python
import functools
import math

import jax
import jax.numpy as jnp
from jax import lax
from jax.experimental import pallas as pl
from jax.sharding import PartitionSpec as P

STEPS = 4
CAP = 2


precise = lax.Precision.HIGHEST


def widen_halo(value, width):
    lat_dim, lon_dim = value.ndim - 1, value.ndim - 2
    for axis, dim, wrap in (("lat", lat_dim, False), ("lon", lon_dim, True)):
        size, length = lax.axis_size(axis), value.shape[dim]
        up = [(i, (i + 1) % size) for i in range(size if wrap else size - 1)]
        down = [(j, i) for i, j in up]
        before = lax.ppermute(lax.slice_in_dim(value, length - width, length, axis=dim), axis, up)
        after = lax.ppermute(lax.slice_in_dim(value, 0, width, axis=dim), axis, down)
        value = jnp.concatenate([before, value, after], axis=dim)
    return value


def face_coeffs(wide, width):
    lat_count = wide.shape[3] - 2 * (width + 1)
    lat_devices = lax.axis_size("lat")
    first = lax.axis_index("lat") * lat_count - width
    cells = first + jnp.arange(lat_count + 2 * width, dtype=jnp.int32)
    inside = ((cells >= 0) & (cells < lat_devices * lat_count)).astype(jnp.float32)
    centre = wide[:, :, 1:-1, 1:-1]
    return (
        inside * (0.5 * (centre + wide[:, :, 1:-1, 2:])),
        inside * (0.5 * (centre + wide[:, :, 1:-1, :-2])),
        inside * (0.5 * (centre + wide[:, :, 2:, 1:-1])),
        inside * (0.5 * (centre + wide[:, :, :-2, 1:-1])),
    )


def diffuse(field, coeffs):
    for sweep in range(STEPS):
        lon_end = field.shape[2] - 1
        lat_end = field.shape[3] - 1
        here = field[:, :, 1:lon_end, 1:lat_end]
        edge = sweep + 1
        north_face, south_face, east_face, west_face = (
            c[:, :, edge : c.shape[2] - edge, edge : c.shape[3] - edge] for c in coeffs
        )
        field = (
            here
            + north_face * (field[:, :, 1:lon_end, 2:] - here)
            + south_face * (field[:, :, 1:lon_end, : lat_end - 1] - here)
            + east_face * (field[:, :, 2:, 1:lat_end] - here)
            + west_face * (field[:, :, : lon_end - 1, 1:lat_end] - here)
        )
    return field


PARTS = 3


def split_parts(value):
    parts = []
    rest = value
    for part in range(PARTS):
        piece = rest.astype(jnp.bfloat16)
        parts.append(piece)
        rest = rest - piece.astype(jnp.float32)
    return parts


def obs_lines(cell_ref, weight_ref, group, lat_count):
    cells = cell_ref[...]
    rows = cells // lat_count
    lats = cells - rows * lat_count
    row_line = jnp.concatenate([rows[g : g + 1, :] for g in range(group)], axis=1)
    lat_line = jnp.concatenate([lats[g : g + 1, :] for g in range(group)], axis=1)
    weights = [
        jnp.concatenate([weight_ref[g, c : c + 1, :] for g in range(group)], axis=1) for c in range(4)
    ]
    return row_line, lat_line, weights


def select_maps(row_line, lat_line, weights, row_count, lat_count):
    width = row_line.shape[1]
    row_ids = lax.broadcasted_iota(jnp.int32, (row_count, width), 0)
    near_rows = (row_ids == row_line).astype(jnp.bfloat16)
    far_rows = (row_ids == row_line + 1).astype(jnp.bfloat16)
    lat_ids = lax.broadcasted_iota(jnp.int32, (lat_count, width), 0)
    near_lat = jnp.where(lat_ids == lat_line, weights[0], 0.0) + jnp.where(
        lat_ids == lat_line + 1, weights[1], 0.0
    )
    far_lat = jnp.where(lat_ids == lat_line, weights[2], 0.0) + jnp.where(
        lat_ids == lat_line + 1, weights[3], 0.0
    )
    return near_rows, far_rows, near_lat, far_lat


def observe_kernel(group, var_count, row_count, lat_count, table_ref, cell_ref, weight_ref, scale_ref, out_ref):
    row_line, lat_line, weights = obs_lines(cell_ref, weight_ref, group, lat_count)
    near_rows, far_rows, near_lat, far_lat = select_maps(row_line, lat_line, weights, row_count, lat_count)
    table = jnp.concatenate(split_parts(table_ref[...]), axis=1)
    near_vals = jnp.dot(table, jnp.concatenate([near_rows] * PARTS, axis=0), preferred_element_type=jnp.float32)
    far_vals = jnp.dot(table, jnp.concatenate([far_rows] * PARTS, axis=0), preferred_element_type=jnp.float32)
    for v in range(var_count):
        span = slice(v * lat_count, (v + 1) * lat_count)
        line = jnp.sum(near_vals[span] * near_lat + far_vals[span] * far_lat, axis=0, keepdims=True)
        for g in range(group):
            out_ref[v, g : g + 1, :] = scale_ref[v, g : g + 1, :] * line[:, g * 128 : (g + 1) * 128]


def spread_kernel(group, var_count, row_count, lat_count, value_ref, cell_ref, weight_ref, out_ref):
    @pl.when(pl.program_id(0) == 0)
    def _():
        out_ref[...] = jnp.zeros_like(out_ref)

    row_line, lat_line, weights = obs_lines(cell_ref, weight_ref, group, lat_count)
    near_rows, far_rows, near_lat, far_lat = select_maps(row_line, lat_line, weights, row_count, lat_count)
    near_parts, far_parts = [], []
    for v in range(var_count):
        line = jnp.concatenate([value_ref[v, g : g + 1, :] for g in range(group)], axis=1)
        near_parts.append(near_lat * line)
        far_parts.append(far_lat * line)
    near_split = split_parts(jnp.concatenate(near_parts, axis=0))
    far_split = split_parts(jnp.concatenate(far_parts, axis=0))
    lhs = jnp.concatenate(near_split + far_split, axis=1)
    rhs = jnp.concatenate([near_rows] * PARTS + [far_rows] * PARTS, axis=1)
    out_ref[...] += lax.dot_general(
        lhs, rhs, (((1,), (1,)), ((), ())), preferred_element_type=jnp.float32
    )


def observe_pallas(field, stencil, bilinear, obs_weight, group=8):
    var_count, level_count, lon_count, lat_count = field.shape
    row_count = level_count * lon_count
    block_count = stencil.shape[0]
    rows_t = jnp.transpose(field.reshape(var_count, row_count, lat_count), (0, 2, 1))
    table = rows_t.reshape(var_count * lat_count, row_count)
    kernel = functools.partial(observe_kernel, group, var_count, row_count, lat_count)
    width = group * stencil.shape[1]
    flops = 2 * 2 * var_count * lat_count * PARTS * row_count * width * (block_count // group)
    return pl.pallas_call(
        kernel,
        grid=(block_count // group,),
        in_specs=[
            pl.BlockSpec(table.shape, lambda i: (0, 0)),
            pl.BlockSpec((group, stencil.shape[1]), lambda i: (i, 0)),
            pl.BlockSpec((group, 4, stencil.shape[1]), lambda i: (i, 0, 0)),
            pl.BlockSpec((var_count, group, stencil.shape[1]), lambda i: (0, i, 0)),
        ],
        out_specs=pl.BlockSpec((var_count, group, stencil.shape[1]), lambda i: (0, i, 0)),
        out_shape=jax.ShapeDtypeStruct(obs_weight.shape, jnp.float32),
        cost_estimate=pl.CostEstimate(flops=flops, transcendentals=0, bytes_accessed=4 * 1024 * 1024),
    )(table, stencil, bilinear, obs_weight)


def spread_pallas(values, stencil, bilinear, field_shape, group=8):
    var_count, level_count, lon_count, lat_count = field_shape
    row_count = level_count * lon_count
    block_count = stencil.shape[0]
    kernel = functools.partial(spread_kernel, group, var_count, row_count, lat_count)
    width = group * stencil.shape[1]
    flops = 2 * 2 * var_count * lat_count * PARTS * row_count * width * (block_count // group)
    total = pl.pallas_call(
        kernel,
        grid=(block_count // group,),
        in_specs=[
            pl.BlockSpec((var_count, group, stencil.shape[1]), lambda i: (0, i, 0)),
            pl.BlockSpec((group, stencil.shape[1]), lambda i: (i, 0)),
            pl.BlockSpec((group, 4, stencil.shape[1]), lambda i: (i, 0, 0)),
        ],
        out_specs=pl.BlockSpec((var_count * lat_count, row_count), lambda i: (0, 0)),
        out_shape=jax.ShapeDtypeStruct((var_count * lat_count, row_count), jnp.float32),
        cost_estimate=pl.CostEstimate(flops=flops, transcendentals=0, bytes_accessed=4 * 1024 * 1024),
    )(values, stencil, bilinear)
    total = jnp.transpose(total.reshape(var_count, lat_count, row_count), (0, 2, 1))
    return total.reshape(field_shape)


def slots_of(block_owner, tile_count):
    targets = block_owner[:, 0]
    block_count = targets.shape[0]
    same_owner = (targets[:, None] == jnp.arange(tile_count, dtype=jnp.int32)[None, :]).astype(
        jnp.int32
    )
    order = jnp.arange(block_count, dtype=jnp.int32)
    lower = (order[:, None] > order[None, :]).astype(jnp.int32)
    earlier = jnp.dot(lower, same_owner)
    rank_within = jnp.sum(earlier * same_owner, axis=1)
    return targets * CAP + rank_within


def mix_blocks(values, correlation):
    return jnp.einsum("vsk,ik->vsi", values, correlation, precision=precise)


def shards(
    increment,
    residual,
    direction,
    diffusivity,
    deviation,
    stencil,
    bilinear,
    obs_weight,
    block_owner,
    correlation,
):
    lat_devices = lax.axis_size("lat")
    lon_devices = lax.axis_size("lon")
    tile_count = lat_devices * lon_devices
    both = widen_halo(jnp.stack([direction, diffusivity]), STEPS + 1)
    coeffs = face_coeffs(both[1], STEPS)

    def apply_diffusion(field):
        return diffuse(widen_halo(field, STEPS), coeffs)

    slots = slots_of(block_owner, tile_count)
    slot_table = (slots[:, None] == jnp.arange(tile_count * CAP, dtype=jnp.int32)[None, :]).astype(
        jnp.float32
    )
    field_shape = direction.shape
    state_field = deviation * diffuse(both[0][:, :, 1:-1, 1:-1], coeffs)
    observed = observe_pallas(state_field, stencil, bilinear, obs_weight)
    buffer = jnp.einsum("vbk,bs->vsk", observed, slot_table, precision=precise)
    returned = lax.all_to_all(
        mix_blocks(
            lax.all_to_all(buffer, ("lat", "lon"), split_axis=1, concat_axis=1, tiled=True),
            correlation,
        ),
        ("lat", "lon"),
        split_axis=1,
        concat_axis=1,
        tiled=True,
    )
    weighted = obs_weight * jnp.einsum("vsk,bs->vbk", returned, slot_table, precision=precise)
    spread_field = deviation * spread_pallas(weighted, stencil, bilinear, field_shape)
    image_field = direction + apply_diffusion(spread_field)
    sums = lax.psum(
        jnp.stack(
            [
                jnp.sum(residual * residual),
                jnp.sum(direction * image_field),
                jnp.sum(residual * image_field),
                jnp.sum(image_field * image_field),
            ]
        ),
        ("lat", "lon"),
    )
    norm_now, curvature, cross, image_norm = sums[0], sums[1], sums[2], sums[3]
    step_size = norm_now / curvature
    increment = increment + step_size * direction
    residual = residual - step_size * image_field
    norm_next = norm_now - 2.0 * step_size * cross + step_size * step_size * image_norm
    direction = residual + norm_next / norm_now * direction
    return (increment, residual, direction)


def solution(mesh):
    in_specs = (
        P(None, None, "lon", "lat"),
        P(None, None, "lon", "lat"),
        P(None, None, "lon", "lat"),
        P(None, None, "lon", "lat"),
        P(None, None, "lon", "lat"),
        P(("lat", "lon"), None),
        P(("lat", "lon"), None, None),
        P(None, ("lat", "lon"), None),
        P(("lat", "lon"), None),
        P(("lat", "lon"), None),
    )
    out_specs = (
        P(None, None, "lon", "lat"),
        P(None, None, "lon", "lat"),
        P(None, None, "lon", "lat"),
    )
    return jax.shard_map(shards, mesh=mesh, in_specs=in_specs, out_specs=out_specs, check_vma=False)
```

time: 609 us -> 294 us (0.48)
  matrix products: 245 us -> 2.8 us
  Pallas kernels: 0 us -> 65.9 us
  local copies, waits for them, and re-layouts: 75.1 us -> 14.7 us
  starting transfers between devices: 73.6 us -> 19.9 us
  other arithmetic: 74.7 us -> 40.6 us
  blocking collectives: 85.8 us -> 95.4 us
    dot_general x64 -> x0, matrix products: 242 us -> none  [the longest x16 67.8 us: add_group(): jnp.einsum('vrk,jk->vrj', near_rows[None] * values[:, None, :], near_lat,...]
    pallas_call x0 -> x2, Pallas kernels: none -> 65.9 us  [the longest x1 34.3 us: spread_pallas(): pl.pallas_call(kernel, grid=(block_count // group,), in_specs=[pl.BlockSp...]
    ppermute x24 -> x8, starting transfers between devices: 68.7 us -> 19.9 us  [the longest x4 12.6 us: widen_halo(): lax.ppermute(lax.slice_in_dim(value, 0, width, axis=dim), axis, down)]
    convert_element_type x48 -> x0, other arithmetic: 31.8 us -> none  [the longest x32 28.7 us: block_maps(): near_rows = (rows == row_base[None, :]).astype(jnp.float32)]
    slice x41 -> x9, local copies, waits for them, and re-layouts: 35.7 us -> 4.16 us  [the longest x6 2.9 us: widen_halo(): lax.slice_in_dim(value, length - width, length, axis=dim)]
    ppermute x24 -> x8, waiting for transfers between devices: 27.5 us -> 43.2 us  [the longest x4 30.2 us: widen_halo(): lax.ppermute(lax.slice_in_dim(value, 0, width, axis=dim), axis, down)]
    all_to_all x0 -> x1, blocking collectives: none -> 15.2 us  [shards(): lax.all_to_all(mix_blocks(lax.all_to_all(buffer, ('lat', 'lon'), split_ax...]
    mul x16 -> x0, local copies, waits for them, and re-layouts: 11.3 us -> none  [add_group(): near_rows[None] * values[:, None, :]]
  transfers between devices with their start and end apart: 25 -> 8, of which waited for: 6 -> 7; matrix products, arithmetic and copies ran while one was open for 2% -> 2% of each run, Pallas kernels for 0% -> 0%
where the time goes in v2:
time: 294 us; the launch traced here: 288 us
  blocking collectives  95.4 us (32%)
  Pallas kernels  65.9 us (22%)
  waiting for transfers between devices  43.2 us (15%)
  other arithmetic  40.6 us (14%)
  starting transfers between devices  19.9 us (7%)
  local copies, waits for them, and re-layouts  14.7 us (5%)
  between operations  5.11 us (2%)
    psum x1, blocking collectives, shards(): lax.psum(jnp.stack([jnp.sum(residual * residual), jnp.sum(direction * ima...  63.8 us
    pallas_call x1, Pallas kernels, spread_pallas(): pl.pallas_call(kernel, grid=(block_count // group,), in_specs=[pl.BlockSp...  34.3 us
    pallas_call x1, Pallas kernels, observe_pallas(): pl.pallas_call(kernel, grid=(block_count // group,), in_specs=[pl.BlockSp...  31.6 us
    ppermute x4, waiting for transfers between devices, widen_halo(): lax.ppermute(lax.slice_in_dim(value, 0, width, axis=dim), axis, down)  30.2 us
    add x6, other arithmetic, diffuse(): here + north_face * (field[:, :, 1:lon_end, 2:] - here)  21.8 us
    all_to_all x1, blocking collectives, shards(): lax.all_to_all(buffer, ('lat', 'lon'), split_axis=1, concat_axis=1, tiled...  16.4 us
    all_to_all x1, blocking collectives, shards(): lax.all_to_all(mix_blocks(lax.all_to_all(buffer, ('lat', 'lon'), split_ax...  15.2 us
    ppermute x4, waiting for transfers between devices, widen_halo(): lax.ppermute(lax.slice_in_dim(value, length - width, length, axis=dim), a...  13 us
  transfers between devices with their start and end apart: 8, of which 7 were waited for; matrix products, arithmetic and copies ran while one was open for 2% of the time, Pallas kernels for 0%

profile of v2, /device:TPU:1, one launch (start us, length us, event | category | flops | bytes accessed | tf_op | source)
XLA Modules:
  0.0 287.7 jit_solution(10394873877154891219)
XLA Ops:
  0.6 1.8 slice_maximum_fusion
  2.8 3.3 %collective-permute-start.1 = (f32[2,2,50,8,5]{2,3,4,1,0:T(8,128)S(1)}, f32[2,2,50,8,5]{2,3,4,1,0:T(8,128)S(1)}, u32[]{:S(2)}, u32[]{:S(2)}) collective-permute-start(f32[2,2,50,8,5]{2,3,4,1,0:T(8,128)S(1)} %copy.56), channel_id=1, source_target_pairs={{16,0},{32,16},{48,32},{64,48},{80,64},{96,80},{112,96},{17,1},{33... | collective-permute-start | bytes 96008 | tf_op jit(solution)/shard_map/ppermute | solution.py:24
  6.5 3.2 %collective-permute-start = (f32[2,2,50,8,5]{2,3,4,1,0:T(8,128)S(1)}, f32[2,2,50,8,5]{2,3,4,1,0:T(8,128)S(1)}, u32[]{:S(2)}, u32[]{:S(2)}) collective-permute-start(f32[2,2,50,8,5]{2,3,4,1,0:T(8,128)S(1)} %copy.55), channel_id=1, source_target_pairs={{0,16},{16,32},{32,48},{48,64},{64,80},{80,96},{96,112},{1,17},{17... | collective-permute-start | bytes 96008 | tf_op jit(solution)/shard_map/ppermute | solution.py:23
  9.8 0.4 copy.58
  10.2 1.0 collective-permute-done
  11.2 0.4 copy.57
  11.7 0.7 pad_maximum_fusion.1
  12.7 0.8 copy.60
  13.5 6.0 %collective-permute-start.3 = (f32[2,2,50,5,138]{4,1,3,2,0:T(2,128)S(1)}, f32[2,2,50,5,138]{4,1,3,2,0:T(2,128)}, u32[]{:S(2)}, u32[]{:S(2)}) collective-permute-start(f32[2,2,50,5,138]{4,1,3,2,0:T(2,128)S(1)} %copy.60), channel_id=1, source_target_pairs={{1,0},{2,1},{3,2},{4,3},{5,4},{6,5},{7,6},{8,7},{9,8},{10,9},{11,1... | collective-permute-start | bytes 1656008 | tf_op jit(solution)/shard_map/ppermute | solution.py:24
  19.5 1.8 copy.59
  21.5 19.7 %collective-permute-done.3 = f32[2,2,50,5,138]{4,1,3,2,0:T(2,128)} collective-permute-done((f32[2,2,50,5,138]{4,1,3,2,0:T(2,128)S(1)}, f32[2,2,50,5,138]{4,1,3,2,0:T(2,128)}, u32[]{:S(2)}, u32[]{:S(2)}) %collective-permute-start.3) | collective-permute-done | bytes 552032 | tf_op jit(solution)/shard_map/ppermute | solution.py:24
  41.2 1.4 copy.62
  42.6 6.2 %collective-permute-done.2 = f32[2,2,50,5,138]{4,1,3,2,0:T(2,128)} collective-permute-done((f32[2,2,50,5,138]{4,1,3,2,0:T(2,128)}, f32[2,2,50,5,138]{4,1,3,2,0:T(2,128)}, u32[]{:S(2)}, u32[]{:S(2)}) %collective-permute-start.2) | collective-permute-done | bytes 552032 | tf_op jit(solution)/shard_map/ppermute | solution.py:23
  48.8 1.4 copy.61
  50.2 2.9 %pad_maximum_fusion = f32[2,2,50,18,138]{4,3,2,1,0:T(8,128)S(1)} fusion(f32[2,2,50,5,138]{4,3,2,1,0:T(8,128)S(1)} %copy.62, f32[2,2,50,8,5]{4,3,2,1,0:T(8,128)S(1)} %copy.58, f32[1,2,50,8,128]{4,3,2,1,0:T(8,128)S(1)} %bitcast.51, f32[1,2,50,8,128]{4,3,2,1,0:T(8,128)S(1)} %bitcast.48, f32[2,2,50,8,5]{4,3,2,1,0:T(8,128)S(1)} %copy.57, ...), kind=kLoop, calls=%fused_computation | loop fusion | flops 2484000 | bytes 3974400 | tf_op jit(solution)/shard_map/concatenate | solution.py:25
  53.5 1.8 fusion.51
  55.3 3.9 %fusion.41 = f32[2,50,14,134]{3,2,1,0:T(8,128)S(1)} fusion(f32[2,50,18,138]{3,2,1,0:T(8,128)S(1)} %get-tuple-element.14, f32[2,50,16,136]{3,2,1,0:T(8,128)S(1)} %get-tuple-element.18, f32[2,50,16,136]{3,2,1,0:T(8,128)S(1)} %get-tuple-element.16, f32[2,50,16,136]{3,2,1,0:T(8,128)S(1)} %get-tuple-element.17, f32[2,50,16,136]{3,2,1,0:T(8,128)S(1)} %get-tuple-element.15), kind=kLoop, calls=%fused_computation.65 | loop fusion | flops 2251200 | bytes 7504000 | tf_op jit(solution)/shard_map/add | solution.py:54
  59.2 3.5 %fusion.33 = f32[2,50,12,132]{3,2,1,0:T(8,128)S(1)} fusion(f32[2,50,14,134]{3,2,1,0:T(8,128)S(1)} %fusion.41, f32[2,50,16,136]{3,2,1,0:T(8,128)S(1)} %get-tuple-element.18, f32[2,50,16,136]{3,2,1,0:T(8,128)S(1)} %get-tuple-element.16, f32[2,50,16,136]{3,2,1,0:T(8,128)S(1)} %get-tuple-element.17, f32[2,50,16,136]{3,2,1,0:T(8,128)S(1)} %get-tuple-element.15), kind=kLoop, calls=%fused_computation.53 | loop fusion | flops 1900800 | bytes 6336000 | tf_op jit(solution)/shard_map/add | solution.py:54
  62.8 3.7 %fusion.25 = f32[2,50,10,130]{3,2,1,0:T(8,128)S(1)} fusion(f32[2,50,12,132]{3,2,1,0:T(8,128)S(1)} %fusion.33, f32[2,50,16,136]{3,2,1,0:T(8,128)S(1)} %get-tuple-element.18, f32[2,50,16,136]{3,2,1,0:T(8,128)S(1)} %get-tuple-element.16, f32[2,50,16,136]{3,2,1,0:T(8,128)S(1)} %get-tuple-element.17, f32[2,50,16,136]{3,2,1,0:T(8,128)S(1)} %get-tuple-element.15), kind=kLoop, calls=%fused_computation.41 | loop fusion | flops 1560000 | bytes 5200000 | tf_op jit(solution)/shard_map/add | solution.py:54
  66.5 1.7 fusion.66
  68.1 2.0 copy.63
  70.1 31.6 %shard_map.121 = f32[2,128,128]{2,1,0:T(8,128)} custom-call(f32[256,400]{1,0:T(8,128)} %bitcast.52, s32[128,128]{1,0:T(8,128)} %cell_ref.3, f32[128,4,128]{2,1,0:T(4,128)} %weight_ref.3, f32[2,128,128]{2,1,0:T(8,128)} %scale_ref.1), custom_call_target="tpu_custom_call" | custom-call | flops 20132659200 | bytes 4194304 | tf_op jit(solution)/shard_map/pallas_call | solution.py:146
  101.7 1.3 convolution_bitcast_fusion
  103.3 16.4 %all_to_all.10 = f32[2,256,128]{2,0,1:T(2,128)S(1)} all-to-all(f32[2,256,128]{2,0,1:T(2,128)S(1)} %copy.65), channel_id=1, replica_groups=mesh['lat'=8,'lon'=16] {'lat','lon'}, dimensions={1} | all-to-all | bytes 524288 | tf_op jit(solution)/shard_map/all_to_all | solution.py:232
  120.3 15.2 %all_to_all.11 = f32[2,256,128]{2,0,1:T(2,128)S(1)} all-to-all(f32[2,256,128]{2,0,1:T(2,128)S(1)} %copy.67), channel_id=1, replica_groups=mesh['lat'=8,'lon'=16] {'lat','lon'}, dimensions={1} | all-to-all | bytes 524288 | tf_op jit(solution)/shard_map/all_to_all | solution.py:230
  135.5 0.9 fusion.52.value_ref
  136.4 34.3 %shard_map.122 = f32[256,400]{1,0:T(8,128)} custom-call(f32[2,128,128]{2,1,0:T(8,128)} %fusion.52.value_ref, s32[128,128]{1,0:T(8,128)} %cell_ref.3, f32[128,4,128]{2,1,0:T(4,128)} %weight_ref.3), custom_call_target="tpu_custom_call" | custom-call | flops 20132659200 | bytes 4194304 | tf_op jit(solution)/shard_map/pallas_call | solution.py:168
  170.7 2.0 copy.69
  172.7 1.2 bitcast_multiply_fusion
  174.1 2.4 collective-permute-start.5
  176.5 3.2 %collective-permute-start.4 = (f32[2,50,8,4]{3,2,1,0:T(8,128)S(1)}, f32[2,50,8,4]{3,2,1,0:T(8,128)S(1)}, u32[]{:S(2)}, u32[]{:S(2)}) collective-permute-start(f32[2,50,8,4]{3,2,1,0:T(8,128)S(1)} %get-tuple-element.26), channel_id=1, source_target_pairs={{0,16},{16,32},{32,48},{48,64},{64,80},{80,96},{96,112},{1,17},{17... | collective-permute-start | bytes 38408 | tf_op jit(solution)/shard_map/ppermute | solution.py:23
  179.7 3.7 %collective-permute-done.5 = f32[2,50,8,4]{3,2,1,0:T(8,128)S(1)} collective-permute-done((f32[2,50,8,4]{3,2,1,0:T(8,128)S(1)}, f32[2,50,8,4]{3,2,1,0:T(8,128)S(1)}, u32[]{:S(2)}, u32[]{:S(2)}) %collective-permute-start.5) | collective-permute-done | bytes 12832 | tf_op jit(solution)/shard_map/ppermute | solution.py:24
  183.4 1.2 collective-permute-done.4
  185.2 0.9 collective-permute-start.7
  186.1 1.0 collective-permute-start.6
  187.1 6.9 %collective-permute-done.7 = f32[2,50,4,136]{3,1,2,0:T(8,128)S(1)} collective-permute-done((f32[2,50,4,136]{3,1,2,0:T(8,128)S(1)}, f32[2,50,4,136]{3,1,2,0:T(8,128)S(1)}, u32[]{:S(2)}, u32[]{:S(2)}) %collective-permute-start.7) | collective-permute-done | bytes 217632 | tf_op jit(solution)/shard_map/ppermute | solution.py:24
  194.1 4.6 %collective-permute-done.6 = f32[2,50,4,136]{3,1,2,0:T(8,128)S(1)} collective-permute-done((f32[2,50,4,136]{3,1,2,0:T(8,128)S(1)}, f32[2,50,4,136]{3,1,2,0:T(8,128)S(1)}, u32[]{:S(2)}, u32[]{:S(2)}) %collective-permute-start.6) | collective-permute-done | bytes 217632 | tf_op jit(solution)/shard_map/ppermute | solution.py:23
  198.9 0.8 pad_maximum_fusion.2
  199.7 0.6 copy-done.2
  200.3 0.5 copy-done.4
  200.8 3.6 %fusion.17 = f32[2,50,14,134]{3,2,1,0:T(8,128)S(1)} fusion(f32[2,50,16,136]{3,2,1,0:T(8,128)S(1)} %pad_maximum_fusion.2, f32[2,50,16,136]{3,2,1,0:T(8,128)S(1)} %copy-done.4, f32[2,50,16,136]{3,2,1,0:T(8,128)S(1)} %get-tuple-element.16, f32[2,50,16,136]{3,2,1,0:T(8,128)S(1)} %copy-done.2, f32[2,50,16,136]{3,2,1,0:T(8,128)S(1)} %get-tuple-element.15), kind=kLoop, calls=%fused_computation.29 | loop fusion | flops 2251200 | bytes 7504000 | tf_op jit(solution)/shard_map/add | solution.py:54
  204.4 3.6 %fusion.9 = f32[2,50,12,132]{3,2,1,0:T(8,128)S(1)} fusion(f32[2,50,14,134]{3,2,1,0:T(8,128)S(1)} %fusion.17, f32[2,50,16,136]{3,2,1,0:T(8,128)S(1)} %copy-done.4, f32[2,50,16,136]{3,2,1,0:T(8,128)S(1)} %get-tuple-element.16, f32[2,50,16,136]{3,2,1,0:T(8,128)S(1)} %copy-done.2, f32[2,50,16,136]{3,2,1,0:T(8,128)S(1)} %get-tuple-element.15), kind=kLoop, calls=%fused_computation.17 | loop fusion | flops 1900800 | bytes 6336000 | tf_op jit(solution)/shard_map/add | solution.py:54
  208.0 3.6 %fusion.1 = f32[2,50,10,130]{3,2,1,0:T(8,128)S(1)} fusion(f32[2,50,12,132]{3,2,1,0:T(8,128)S(1)} %fusion.9, f32[2,50,16,136]{3,2,1,0:T(8,128)S(1)} %copy-done.4, f32[2,50,16,136]{3,2,1,0:T(8,128)S(1)} %get-tuple-element.16, f32[2,50,16,136]{3,2,1,0:T(8,128)S(1)} %copy-done.2, f32[2,50,16,136]{3,2,1,0:T(8,128)S(1)} %get-tuple-element.15), kind=kLoop, calls=%fused_computation.5 | loop fusion | flops 1560000 | bytes 5200000 | tf_op jit(solution)/shard_map/add | solution.py:54
  211.5 2.5 multiply_reduce_fusion.3
  214.0 2.6 pad_maximum_fusion.5
  216.6 63.8 %psum.7 = f32[4]{0:T(128)S(1)} all-reduce(f32[4]{0:T(128)S(1)} %pad_maximum_fusion.5), channel_id=1, replica_groups=mesh['lat'=8,'lon'=16] {'lat','lon'}, use_global_device_ids=true, to_apply=%region_5.0 | all-reduce | flops 4 | bytes 32 | tf_op jit(solution)/shard_map/psum | solution.py:243
  280.5 0.7 fusion.88
  285.0 2.5 multiply_add_fusion
  (41 shorter events, 3.6 us)
Async XLA Ops:
  0.6 119.0 %copy-start = (f32[128,128]{1,0:T(8,128)S(1)}, f32[128,128]{1,0:T(8,128)}, u32[]{:S(2)}) copy-start(f32[128,128]{1,0:T(8,128)} %param.19) | copy-start | bytes 196612
  2.4 9.2 %copy-start.5 = (f32[2,50,8,128]{3,2,1,0:T(8,128)S(1)}, f32[2,50,8,128]{3,2,1,0:T(8,128)}, u32[]{:S(2)}) copy-start(f32[2,50,8,128]{3,2,1,0:T(8,128)} %param.12) | copy-start | bytes 1228804
  2.4 9.2 %copy-start.7 = (f32[2,50,8,128]{3,2,1,0:T(8,128)S(1)}, f32[2,50,8,128]{3,2,1,0:T(8,128)}, u32[]{:S(2)}) copy-start(f32[2,50,8,128]{3,2,1,0:T(8,128)} %param.13) | copy-start | bytes 1228804
  2.8 6.9 %collective-permute-start.1 = (f32[2,2,50,8,5]{2,3,4,1,0:T(8,128)S(1)}, f32[2,2,50,8,5]{2,3,4,1,0:T(8,128)S(1)}, u32[]{:S(2)}, u32[]{:S(2)}) collective-permute-start(f32[2,2,50,8,5]{2,3,4,1,0:T(8,128)S(1)} %copy.56), channel_id=1, source_target_pairs={{16,0},{32,16},{48,32},{64,48},{80,64},{96,80},{112,96},{17,1},{33... | collective-permute-start | bytes 96008 | tf_op jit(solution)/shard_map/ppermute | solution.py:24
  6.5 4.7 %collective-permute-start = (f32[2,2,50,8,5]{2,3,4,1,0:T(8,128)S(1)}, f32[2,2,50,8,5]{2,3,4,1,0:T(8,128)S(1)}, u32[]{:S(2)}, u32[]{:S(2)}) collective-permute-start(f32[2,2,50,8,5]{2,3,4,1,0:T(8,128)S(1)} %copy.55), channel_id=1, source_target_pairs={{0,16},{16,32},{32,48},{48,64},{64,80},{80,96},{96,112},{1,17},{17... | collective-permute-start | bytes 96008 | tf_op jit(solution)/shard_map/ppermute | solution.py:23
  13.5 7.9 %copy-start.11 = (s32[128,1]{0,1:T(1,128)S(1)}, s32[128,1]{0,1:T(1,128)}, u32[]{:S(2)}) copy-start(s32[128,1]{0,1:T(1,128)} %param.18) | copy-start | bytes 1540
  13.5 27.7 %collective-permute-start.3 = (f32[2,2,50,5,138]{4,1,3,2,0:T(2,128)S(1)}, f32[2,2,50,5,138]{4,1,3,2,0:T(2,128)}, u32[]{:S(2)}, u32[]{:S(2)}) collective-permute-start(f32[2,2,50,5,138]{4,1,3,2,0:T(2,128)S(1)} %copy.60), channel_id=1, source_target_pairs={{1,0},{2,1},{3,2},{4,3},{5,4},{6,5},{7,6},{8,7},{9,8},{10,9},{11,1... | collective-permute-start | bytes 1656008 | tf_op jit(solution)/shard_map/ppermute | solution.py:24
  21.3 27.5 %collective-permute-start.2 = (f32[2,2,50,5,138]{4,1,3,2,0:T(2,128)}, f32[2,2,50,5,138]{4,1,3,2,0:T(2,128)}, u32[]{:S(2)}, u32[]{:S(2)}) collective-permute-start(f32[2,2,50,5,138]{4,1,3,2,0:T(2,128)} %copy.59), channel_id=1, source_target_pairs={{0,1},{1,2},{2,3},{3,4},{4,5},{5,6},{6,7},{7,8},{8,9},{9,10},{10,1... | collective-permute-start | bytes 1656008 | tf_op jit(solution)/shard_map/ppermute | solution.py:23
  55.3 11.2 %copy-start.1 = (f32[2,50,16,136]{3,2,1,0:T(8,128)}, f32[2,50,16,136]{3,2,1,0:T(8,128)S(1)}, u32[]{:S(2)}) copy-start(f32[2,50,16,136]{3,2,1,0:T(8,128)S(1)} %get-tuple-element.17) | copy-start | bytes 2611204
  55.3 11.2 %copy-start.3 = (f32[2,50,16,136]{3,2,1,0:T(8,128)}, f32[2,50,16,136]{3,2,1,0:T(8,128)S(1)}, u32[]{:S(2)}) copy-start(f32[2,50,16,136]{3,2,1,0:T(8,128)S(1)} %get-tuple-element.18) | copy-start | bytes 2611204
  62.7 3.7 %copy-start.8 = (f32[2,50,8,128]{3,2,1,0:T(8,128)S(1)}, f32[2,50,8,128]{3,2,1,0:T(8,128)}, u32[]{:S(2)}) copy-start(f32[2,50,8,128]{3,2,1,0:T(8,128)} %param.14) | copy-start | bytes 1228804
  101.7 33.8 %copy-start.10 = (f32[2,128,128]{2,1,0:T(8,128)S(1)}, f32[2,128,128]{2,1,0:T(8,128)}, u32[]{:S(2)}) copy-start(f32[2,128,128]{2,1,0:T(8,128)} %scale_ref.1) | copy-start | bytes 393220
  174.1 9.3 %collective-permute-start.5 = (f32[2,50,8,4]{3,2,1,0:T(8,128)S(1)}, f32[2,50,8,4]{3,2,1,0:T(8,128)S(1)}, u32[]{:S(2)}, u32[]{:S(2)}) collective-permute-start(f32[2,50,8,4]{3,2,1,0:T(8,128)S(1)} %get-tuple-element.27), channel_id=1, source_target_pairs={{16,0},{32,16},{48,32},{64,48},{80,64},{96,80},{112,96},{17,1},{33... | collective-permute-start | bytes 38408 | tf_op jit(solution)/shard_map/ppermute | solution.py:24
  176.5 8.1 %collective-permute-start.4 = (f32[2,50,8,4]{3,2,1,0:T(8,128)S(1)}, f32[2,50,8,4]{3,2,1,0:T(8,128)S(1)}, u32[]{:S(2)}, u32[]{:S(2)}) collective-permute-start(f32[2,50,8,4]{3,2,1,0:T(8,128)S(1)} %get-tuple-element.26), channel_id=1, source_target_pairs={{0,16},{16,32},{32,48},{48,64},{64,80},{80,96},{96,112},{1,17},{17... | collective-permute-start | bytes 38408 | tf_op jit(solution)/shard_map/ppermute | solution.py:23
  185.2 8.8 %collective-permute-start.7 = (f32[2,50,4,136]{3,1,2,0:T(8,128)S(1)}, f32[2,50,4,136]{3,1,2,0:T(8,128)S(1)}, u32[]{:S(2)}, u32[]{:S(2)}) collective-permute-start(f32[2,50,4,136]{3,1,2,0:T(8,128)S(1)} %copy.71), channel_id=1, source_target_pairs={{1,0},{2,1},{3,2},{4,3},{5,4},{6,5},{7,6},{8,7},{9,8},{10,9},{11,1... | collective-permute-start | bytes 652808 | tf_op jit(solution)/shard_map/ppermute | solution.py:24
  186.1 12.6 %collective-permute-start.6 = (f32[2,50,4,136]{3,1,2,0:T(8,128)S(1)}, f32[2,50,4,136]{3,1,2,0:T(8,128)S(1)}, u32[]{:S(2)}, u32[]{:S(2)}) collective-permute-start(f32[2,50,4,136]{3,1,2,0:T(8,128)S(1)} %copy.70), channel_id=1, source_target_pairs={{0,1},{1,2},{2,3},{3,4},{4,5},{5,6},{6,7},{7,8},{8,9},{9,10},{10,1... | collective-permute-start | bytes 652808 | tf_op jit(solution)/shard_map/ppermute | solution.py:23
  198.9 1.4 copy-start.2
  198.9 1.9 copy-start.4
  207.9 3.6 %copy-start.6 = (f32[2,50,8,128]{3,2,1,0:T(8,128)S(1)}, f32[2,50,8,128]{3,2,1,0:T(8,128)}, u32[]{:S(2)}) copy-start(f32[2,50,8,128]{3,2,1,0:T(8,128)} %param.12) | copy-start | bytes 1228804
  207.9 3.6 %copy-start.9 = (f32[2,50,8,128]{3,2,1,0:T(8,128)S(1)}, f32[2,50,8,128]{3,2,1,0:T(8,128)}, u32[]{:S(2)}) copy-start(f32[2,50,8,128]{3,2,1,0:T(8,128)} %param.11) | copy-start | bytes 1228804
